TPU v7x, 512 devices: a whole 4x8x8 slice. The times are simulated.
512 devices in a mesh: layer: 256 (over z, y, x_lo, core), rhs: 2 (over x_hi).
Axes of the slice: x: 4 (x_hi: 2, x_lo: 2; x = x_hi * 2 + x_lo), y: 8, z: 8, core: 2. Of those that a mesh axis runs over, the one named last changes fastest.
Arguments:
- diag_block: float32 [512, 384, 384], P('layer'), may hold values from -0.234742767 to 4.6347428, as said below
- coupling: float32 [512, 384, 384], P('layer'), may hold values from -1.76123724 to 1.76123724
- right_side: float32 [512, 384, 256], P('layer', None, 'rhs'), may hold values from -6 to 6
Outputs:
- inverse_out: float32 [512, 384, 384], P('layer')
- rhs_out: float32 [512, 384, 256], P('layer', None, 'rhs')
Inputs may be any that keep to these rules, and one draw needn't show every extreme that they name: `diag_block`: each diagonal block is symmetric.
All inputs are finite; a program needn't handle non-finite values.
Results may differ from a plain program's by a relative error of at most 0.00013.
Values sent between devices are 32-bit elements; how exact they have to be, the bound alone decides.
No kernel may reach another device: no remote copies, remote signals or barrier semaphores. Data moves between devices by JAX's collectives and lax.ppermute only.
A program may use at most 64 MiB of HBM per device.

v0:
```python
import jax
import jax.numpy as jnp
from jax import lax
from jax.experimental import pallas as pl
from jax.experimental.pallas import tpu as pltpu
from jax.sharding import PartitionSpec as P


F32 = jnp.float32
BF16 = jnp.bfloat16
N = 384
C = 128
W = 2 * N + C
MIB = 1 << 20


def eye():
    rows = lax.broadcasted_iota(jnp.int32, (N, N), 0)
    return rows == lax.broadcasted_iota(jnp.int32, (N, N), 1)


def halves(x):
    high = x.astype(BF16)
    return high, (x - high.astype(F32)).astype(BF16)


def put_left(ref, x):
    high, low = halves(x)
    ref[:, 0:N] = high
    ref[:, N : 2 * N] = high
    ref[:, 2 * N : 3 * N] = low


def put_right(ref, x, at=0):
    high, low = halves(x)
    cols = slice(at, at + x.shape[1])
    ref[0:N, cols] = high
    ref[N : 2 * N, cols] = low
    ref[2 * N : 3 * N, cols] = high


def put_right_t(ref, x):
    high, low = halves(x)
    ref[:, 0:N] = high
    ref[:, N : 2 * N] = low
    ref[:, 2 * N : 3 * N] = high


def dot(left, right):
    return jnp.dot(left, right, preferred_element_type=F32)


def dot_t(left, right):
    return lax.dot_general(
        left, right, (((1,), (1,)), ((), ())), preferred_element_type=F32
    )


def invert(block, out, left_e, left_p, right_e, right_p, s_e, s_2):
    scale = N / jnp.sum(jnp.where(eye(), block[...], 0.0))
    s_e[...] = jnp.where(eye(), 1.0, 0.0) - scale * block[...]
    put_left(left_e, s_e[...])
    put_right(right_e, s_e[...])
    s_2[...] = dot(left_e[...], right_e[...])
    put_left(left_p, s_2[...])
    put_right(right_p, s_2[...])
    put_right(right_e, dot(left_p[...], right_p[...]))
    cube = dot(left_e[...], right_p[...])
    s_e[...] = jnp.where(eye(), 1.0, 0.0) + s_e[...] + s_2[...] + cube
    put_left(left_p, s_e[...])
    out[...] = scale * (s_e[...] + dot(left_p[...], right_e[...]))


INVERT_SCRATCH = [
    pltpu.VMEM((N, 3 * N), BF16),
    pltpu.VMEM((N, 3 * N), BF16),
    pltpu.VMEM((3 * N, N), BF16),
    pltpu.VMEM((3 * N, N), BF16),
    pltpu.VMEM((N, N), F32),
    pltpu.VMEM((N, N), F32),
]


def first_kernel(diag, coup, rhs, both, inv_out, rhs_out, d_in, u_in, r_in, x_s, right, left, tmp, *rest):
    inv_scratch, sems = rest[:6], rest[6]
    core = lax.axis_index("layer") % 2
    loads = [
        pltpu.make_async_copy(diag.at[0], d_in.at[0], sems.at[0]),
        pltpu.make_async_copy(coup.at[0], u_in, sems.at[1]),
        pltpu.make_async_copy(rhs.at[0], r_in.at[0], sems.at[2]),
        pltpu.make_async_copy(diag.at[1], d_in.at[1], sems.at[3]),
        pltpu.make_async_copy(coup.at[1], both.at[core, :, N : 2 * N], sems.at[4]),
        pltpu.make_async_copy(rhs.at[1], r_in.at[1], sems.at[5]),
    ]
    for load in loads:
        load.start()
    loads[0].wait()
    invert(d_in.at[0], x_s, *inv_scratch)
    for load in loads[1:]:
        load.wait()
    stores = [
        pltpu.make_async_copy(x_s, inv_out.at[0], sems.at[0]),
        pltpu.make_async_copy(r_in.at[0], rhs_out.at[0], sems.at[1]),
    ]
    for store in stores:
        store.start()
    both[1 - core, :, 0:N] = x_s[...]
    put_left(left, x_s[...])
    put_right(right, u_in[...], 0)
    put_right(right, r_in[0], N)
    tmp[...] = dot(left[...], right[...])
    both[1 - core, :, N:W] = tmp[...]
    put_left(left, u_in[...].T)
    put_right(right, tmp[...])
    tmp[...] = dot(left[...], right[...])
    both[core, :, 0:N] = d_in[1] - tmp[:, 0:N]
    both[core, :, 2 * N : W] = r_in[1] - tmp[:, N : N + C]
    for store in stores:
        store.wait()


def second_kernel(both, recv, x_b, u_b, r_b, left, right, right_t, d_s, tmp, *inv_scratch):
    at_low = (lax.axis_index("layer") % 2) == 0
    u_s = jnp.where(at_low, both[0, :, N : 2 * N], recv[:, N : 2 * N])
    put_left(left, u_s)
    put_right_t(right_t, u_s)
    put_right(right, jnp.where(at_low, recv[...], both[0]))
    tmp[...] = dot(left[...], right[...])
    put_left(left, tmp[:, 0:N])
    d_old = jnp.where(at_low, both[0, :, 0:N], recv[:, 0:N])
    d_s[...] = d_old - dot_t(left[...], right_t[...])
    u_b[...] = -tmp[:, N : 2 * N]
    r_b[...] = jnp.where(at_low, both[0, :, 2 * N : W], recv[:, 2 * N : W]) - tmp[:, 2 * N : W]
    invert(d_s, x_b, *inv_scratch)


def third_kernel(
    both, x_b, u_b, r_b, u_l, inv_in, rhs_in, pay, full, inv_out, rhs_out, left, right, right_t, acc, tmp, w_s, sems
):
    del inv_in, rhs_in
    at_low = (lax.axis_index("layer") % 2) == 0
    stores = [
        pltpu.make_async_copy(x_b, inv_out.at[1], sems.at[0]),
        pltpu.make_async_copy(r_b, rhs_out.at[1], sems.at[1]),
    ]

    @pl.when(at_low)
    def _():
        for store in stores:
            store.start()
        put_left(left, u_l[...])
        put_right_t(right_t, u_l[...])
        put_right(right, both[1])
        tmp[...] = dot(left[...], right[...])
        put_left(left, tmp[:, 0:N])
        acc[:, 0:N] = dot_t(left[...], right_t[...])
        acc[:, N : N + C] = tmp[:, 2 * N : W]
        w_s[...] = -tmp[:, N : 2 * N]

    @pl.when(jnp.logical_not(at_low))
    def _():
        w_s[...] = u_b[...].T
        acc[:, 0:N] = -both[1, :, 0:N]
        acc[:, N : N + C] = -both[1, :, 2 * N : W]

    put_left(left, w_s[...])
    put_right_t(right_t, w_s[...])
    put_right(right, x_b[...])
    put_left(left, dot(left[...], right[:, 0:N]))
    put_right(right, u_b[...], 0)
    put_right(right, r_b[...], N)
    sign = jnp.where(at_low, 1.0, -1.0)
    pay[:, 0:N] = sign * (acc[:, 0:N] + dot_t(left[...], right_t[...]))
    tmp[:, 0 : N + C] = dot(left[...], right[:, 0 : N + C])
    pay[:, N : N + C] = sign * (acc[:, N : N + C] + tmp[:, N : N + C])

    @pl.when(at_low)
    def _():
        full[:, 0 : N + C] = pay[...]
        full[:, N + C : W] = -tmp[:, 0:N]
        for store in stores:
            store.wait()


def fourth_kernel(
    pay, other, full, inv_in, rhs_in, out, inv_out, rhs_out, left, right, right_t, d_s, x_s, r_s, w_s, *rest
):
    del inv_in, rhs_in
    inv_scratch, sems = rest[:6], rest[6]
    place = lax.axis_index("layer") % 4
    at_first = place == 1
    stores = [
        pltpu.make_async_copy(x_s, inv_out.at[1], sems.at[0]),
        pltpu.make_async_copy(r_s, rhs_out.at[1], sems.at[1]),
    ]

    @pl.when(place % 2 == 1)
    def _():
        mine = jnp.where(at_first, pay[...], other[...])
        theirs = jnp.where(at_first, other[...], full[:, 0 : N + C])
        d_s[...] = mine[:, 0:N] - theirs[:, 0:N]
        r_s[...] = mine[:, N : N + C] - theirs[:, N : N + C]
        invert(d_s, x_s, *inv_scratch)

        @pl.when(at_first)
        def _():
            for store in stores:
                store.start()
            w_s[...] = full[:, N + C : W]

        @pl.when(jnp.logical_not(at_first))
        def _():
            w_s[...] = full[:, N + C : W].T

        put_left(left, w_s[...])
        put_right_t(right_t, w_s[...])
        put_right(right, x_s[...])
        put_left(left, dot(left[...], right[...]))
        put_right(right, r_s[...])
        o_d = dot_t(left[...], right_t[...])
        out[:, 0:N] = jnp.where(at_first, full[:, 0:N] + o_d, pay[:, 0:N] - o_d)
        o_r = dot(left[...], right[:, 0:C])
        out[:, N : N + C] = jnp.where(at_first, full[:, N : N + C] + o_r, pay[:, N : N + C] - o_r)

        @pl.when(at_first)
        def _():
            for store in stores:
                store.wait()


def last_kernel(pay, other, inv_in, rhs_in, inv_out, rhs_out, d_s, x_s, r_s, *rest):
    del inv_in, rhs_in
    inv_scratch, sems = rest[:6], rest[6]

    @pl.when(lax.axis_index("layer") % 4 == 3)
    def _():
        r_s[...] = pay[:, N : N + C] - other[:, N : N + C]
        rhs_store = pltpu.make_async_copy(r_s, rhs_out.at[1], sems.at[1])
        rhs_store.start()
        d_s[...] = pay[:, 0:N] - other[:, 0:N]
        invert(d_s, x_s, *inv_scratch)
        inv_store = pltpu.make_async_copy(x_s, inv_out.at[1], sems.at[0])
        inv_store.start()
        inv_store.wait()
        rhs_store.wait()


def vmem():
    return pl.BlockSpec(memory_space=pltpu.VMEM)


def in_hbm():
    return pl.BlockSpec(memory_space=pltpu.HBM)


def like(*shape):
    return jax.ShapeDtypeStruct(shape, F32)


def call(kernel, outs, out_specs, in_specs, scratch, products, aliases=None):
    return pl.pallas_call(
        kernel,
        out_shape=outs,
        in_specs=in_specs,
        out_specs=out_specs,
        scratch_shapes=scratch,
        input_output_aliases=aliases or {},
        compiler_params=pltpu.CompilerParams(vmem_limit_bytes=28 * MIB),
        cost_estimate=pl.CostEstimate(
            flops=int(products * 6 * N * N * N), bytes_accessed=4 * MIB, transcendentals=0
        ),
    )


def reduce_chain(diag_block, coupling, right_side):
    size = lax.axis_size("layer")
    groups = range(size // 4)

    def send(block, route):
        return lax.ppermute(block, "layer", [(i % size, j % size) for i, j in route])

    wide = pltpu.VMEM((3 * N, W), BF16)
    mid = pltpu.VMEM((3 * N, N + C), BF16)
    flat = pltpu.VMEM((N, 3 * N), BF16)
    tile = pltpu.VMEM((N, N), F32)
    thin = pltpu.VMEM((N, C), F32)
    sems = pltpu.SemaphoreType.DMA((6,))
    outputs = (like(2, N, N), like(2, N, C))

    u_left = send(coupling[1], [(i, i + 1) for i in range(1, size, 2)])
    both, inv_out, rhs_out = call(
        first_kernel,
        (like(2, N, W), *outputs),
        (vmem(), in_hbm(), in_hbm()),
        [in_hbm()] * 3,
        [
            pltpu.VMEM((2, N, N), F32),
            tile,
            pltpu.VMEM((2, N, C), F32),
            tile,
            mid,
            flat,
            pltpu.VMEM((N, N + C), F32),
            *INVERT_SCRATCH,
            sems,
        ],
        6.67,
    )(*[pltpu.with_memory_space_constraint(x, pltpu.HBM) for x in (diag_block, coupling, right_side)])
    recv = send(both[0], [(i, i ^ 1) for i in range(size)])
    x_b, u_b, r_b = call(
        second_kernel,
        (like(N, N), like(N, N), like(N, C)),
        (vmem(), vmem(), vmem()),
        [vmem()] * 2,
        [flat, wide, flat, tile, pltpu.VMEM((N, W), F32), *INVERT_SCRATCH],
        7.33,
    )(both, recv)
    pay, full, inv_out, rhs_out = call(
        third_kernel,
        (like(N, N + C), like(N, W), *outputs),
        (vmem(), vmem(), in_hbm(), in_hbm()),
        [vmem()] * 5 + [in_hbm()] * 2,
        [flat, wide, flat, pltpu.VMEM((N, N + C), F32), pltpu.VMEM((N, W), F32), tile, sems],
        6.67,
        {5: 2, 6: 3},
    )(both, x_b, u_b, r_b, u_left, inv_out, rhs_out)
    across = [(4 * g + 1, 4 * g + 3) for g in groups] + [(4 * g + 2, 4 * g + 1) for g in groups]
    other = send(pay, across)
    full = send(full, [(i, i + 1) for i in range(0, size, 2)])
    out, inv_out, rhs_out = call(
        fourth_kernel,
        (like(N, N + C), *outputs),
        (vmem(), in_hbm(), in_hbm()),
        [vmem()] * 3 + [in_hbm()] * 2,
        [flat, pltpu.VMEM((3 * N, N), BF16), flat, tile, tile, thin, tile, *INVERT_SCRATCH, sems],
        6.33,
        {3: 1, 4: 2},
    )(pay, other, full, inv_out, rhs_out)
    last = send(out, [(4 * g + 5, 4 * g + 3) for g in groups])
    return call(
        last_kernel,
        outputs,
        (in_hbm(), in_hbm()),
        [vmem()] * 2 + [in_hbm()] * 2,
        [tile, tile, thin, *INVERT_SCRATCH, sems],
        4,
        {2: 0, 3: 1},
    )(out, last, inv_out, rhs_out)


def solution(mesh):
    return jax.shard_map(
        reduce_chain,
        mesh=mesh,
        in_specs=(P("layer", None, None), P("layer", None, None), P("layer", None, "rhs")),
        out_specs=(P("layer", None, None), P("layer", None, "rhs")),
        check_vma=False,
    )
```

profile of v0, /device:TPU:1, one launch (start us, length us, event | category | flops | bytes accessed | tf_op | source)
XLA Modules:
  0.0 63.2 jit_solution(6073958164265242358)
XLA Ops:
  0.6 5.2 %shard_map.50 = (f32[2,384,896]{2,1,0:T(8,128)S(1)}, f32[2,384,384]{2,1,0:T(8,128)}, f32[2,384,128]{2,1,0:T(8,128)}) custom-call(f32[2,384,384]{2,1,0:T(8,128)} %diag.1, f32[2,384,384]{2,1,0:T(8,128)} %coup.1, f32[2,384,128]{2,1,0:T(8,128)} %rhs.1), custom_call_target="tpu_custom_call" | custom-call | flops 2266056704 | bytes 4194304 | tf_op jit(solution)/shard_map/pallas_call | solution.py:291
  5.8 0.0 copy-start
  5.9 0.1 slice_bitcast_fusion
  6.0 8.9 %collective-permute-start = (f32[384,896]{1,0:T(8,128)S(1)}, f32[384,896]{1,0:T(8,128)S(1)}, u32[]{:S(2)}, u32[]{:S(2)}) collective-permute-start(f32[384,896]{1,0:T(8,128)S(1)} %slice_bitcast_fusion), channel_id=1, source_target_pairs={{0,2},{2,0},{4,6},{6,4},{8,10},{10,8},{12,14},{14,12},{16,18},{18,... | collective-permute-start | bytes 4128776 | tf_op jit(solution)/shard_map/ppermute | solution.py:280
  14.8 0.0 copy-done
  14.9 1.3 %collective-permute-start.1 = (f32[384,384]{1,0:T(8,128)S(1)}, f32[384,384]{1,0:T(8,128)S(1)}, u32[]{:S(2)}, u32[]{:S(2)}) collective-permute-start(f32[384,384]{1,0:T(8,128)S(1)} %slice_bitcast_fusion.1), channel_id=1, source_target_pairs={{2,4},{6,8},{10,12},{14,16},{18,20},{22,24},{26,28},{30,32},{34,36... | collective-permute-start | bytes 1769480 | tf_op jit(solution)/shard_map/ppermute | solution.py:280
  16.2 1.3 %collective-permute-done.recv = f32[384,896]{1,0:T(8,128)S(1)} collective-permute-done((f32[384,896]{1,0:T(8,128)S(1)}, f32[384,896]{1,0:T(8,128)S(1)}, u32[]{:S(2)}, u32[]{:S(2)}) %collective-permute-start) | collective-permute-done | bytes 1376288 | tf_op jit(solution)/shard_map/ppermute | solution.py:280
  17.6 4.7 %shard_map.51 = (f32[384,384]{1,0:T(8,128)S(1)}, f32[384,384]{1,0:T(8,128)S(1)}, f32[384,128]{1,0:T(8,128)S(1)}) custom-call(f32[2,384,896]{2,1,0:T(8,128)S(1)} %get-tuple-element.15.both, f32[384,896]{1,0:T(8,128)S(1)} %collective-permute-done.recv), custom_call_target="tpu_custom_call" | custom-call | flops 2490284032 | bytes 4194304 | tf_op jit(solution)/shard_map/pallas_call | solution.py:310
  22.3 0.7 %collective-permute-done.1.u_l = f32[384,384]{1,0:T(8,128)S(1)} collective-permute-done((f32[384,384]{1,0:T(8,128)S(1)}, f32[384,384]{1,0:T(8,128)S(1)}, u32[]{:S(2)}, u32[]{:S(2)}) %collective-permute-start.1) | collective-permute-done | bytes 589856 | tf_op jit(solution)/shard_map/ppermute | solution.py:280
  23.0 2.2 %shard_map.52 = (f32[384,512]{1,0:T(8,128)S(1)}, f32[384,896]{1,0:T(8,128)S(1)}, f32[2,384,384]{2,1,0:T(8,128)}, f32[2,384,128]{2,1,0:T(8,128)}) custom-call(f32[2,384,896]{2,1,0:T(8,128)S(1)} %get-tuple-element.15.both, f32[384,384]{1,0:T(8,128)S(1)} %get-tuple-element.16.x_b, ...), custom_call_target="tpu_custom_call", output_to_operand_aliasing={{2}: (5, {}), {3}: (6, {})} | custom-call | flops 2266056704 | bytes 4194304 | tf_op jit(solution)/shard_map/pallas_call | solution.py:318
  25.2 1.3 %collective-permute-start.3 = (f32[384,896]{1,0:T(8,128)S(1)}, f32[384,896]{1,0:T(8,128)S(1)}, u32[]{:S(2)}, u32[]{:S(2)}) collective-permute-start(f32[384,896]{1,0:T(8,128)S(1)} %get-tuple-element.22), channel_id=1, source_target_pairs={{0,2},{4,6},{8,10},{12,14},{16,18},{20,22},{24,26},{28,30},{32,34}... | collective-permute-start | bytes 4128776 | tf_op jit(solution)/shard_map/ppermute | solution.py:280
  26.5 1.9 %collective-permute-start.2 = (f32[384,512]{1,0:T(8,128)S(1)}, f32[384,512]{1,0:T(8,128)S(1)}, u32[]{:S(2)}, u32[]{:S(2)}) collective-permute-start(f32[384,512]{1,0:T(8,128)S(1)} %get-tuple-element.21.pay), channel_id=1, source_target_pairs={{2,6},{10,14},{18,22},{26,30},{34,38},{42,46},{50,54},{58,62},{66,... | collective-permute-start | bytes 2359304 | tf_op jit(solution)/shard_map/ppermute | solution.py:280
  28.4 13.2 %collective-permute-done.2.other = f32[384,512]{1,0:T(8,128)S(1)} collective-permute-done((f32[384,512]{1,0:T(8,128)S(1)}, f32[384,512]{1,0:T(8,128)S(1)}, u32[]{:S(2)}, u32[]{:S(2)}) %collective-permute-start.2) | collective-permute-done | bytes 786464 | tf_op jit(solution)/shard_map/ppermute | solution.py:280
  41.6 0.0 collective-permute-done.3.full
  41.6 4.9 %shard_map.53 = (f32[384,512]{1,0:T(8,128)S(1)}, f32[2,384,384]{2,1,0:T(8,128)}, f32[2,384,128]{2,1,0:T(8,128)}) custom-call(f32[384,512]{1,0:T(8,128)S(1)} %get-tuple-element.21.pay, f32[384,512]{1,0:T(8,128)S(1)} %collective-permute-done.2.other, f32[384,896]{1,0:T(8,128)S(1)} %collective-permute-done.3.full, ...), custom_call_target="tpu_custom_call", output_to_operand_aliasing={{1}: (3, {}), {2}: (4, {})} | custom-call | flops 2150545408 | bytes 4194304 | tf_op jit(solution)/shard_map/pallas_call | solution.py:330
  46.5 7.5 %collective-permute-start.4 = (f32[384,512]{1,0:T(8,128)S(1)}, f32[384,512]{1,0:T(8,128)S(1)}, u32[]{:S(2)}, u32[]{:S(2)}) collective-permute-start(f32[384,512]{1,0:T(8,128)S(1)} %get-tuple-element.25.pay), channel_id=1, source_target_pairs={{10,6},{18,14},{26,22},{34,30},{42,38},{50,46},{58,54},{66,62},{74... | collective-permute-start | bytes 2359304 | tf_op jit(solution)/shard_map/ppermute | solution.py:280
  54.1 8.9 %collective-permute-done.4.other = f32[384,512]{1,0:T(8,128)S(1)} collective-permute-done((f32[384,512]{1,0:T(8,128)S(1)}, f32[384,512]{1,0:T(8,128)S(1)}, u32[]{:S(2)}, u32[]{:S(2)}) %collective-permute-start.4) | collective-permute-done | bytes 786464 | tf_op jit(solution)/shard_map/ppermute | solution.py:280
  62.9 0.1 shard_map.54
  (1 shorter events, 0.0 us)
Async XLA Ops:
  5.8 9.0 %copy-start = (f32[2,384,384]{2,1,0:T(8,128)S(1)}, f32[2,384,384]{2,1,0:T(8,128)}, u32[]{:S(2)}) copy-start(f32[2,384,384]{2,1,0:T(8,128)} %coup.1) | copy-start | bytes 3538948
  6.0 11.6 %collective-permute-start = (f32[384,896]{1,0:T(8,128)S(1)}, f32[384,896]{1,0:T(8,128)S(1)}, u32[]{:S(2)}, u32[]{:S(2)}) collective-permute-start(f32[384,896]{1,0:T(8,128)S(1)} %slice_bitcast_fusion), channel_id=1, source_target_pairs={{0,2},{2,0},{4,6},{6,4},{8,10},{10,8},{12,14},{14,12},{16,18},{18,... | collective-permute-start | bytes 4128776 | tf_op jit(solution)/shard_map/ppermute | solution.py:280
  14.9 8.1 %collective-permute-start.1 = (f32[384,384]{1,0:T(8,128)S(1)}, f32[384,384]{1,0:T(8,128)S(1)}, u32[]{:S(2)}, u32[]{:S(2)}) collective-permute-start(f32[384,384]{1,0:T(8,128)S(1)} %slice_bitcast_fusion.1), channel_id=1, source_target_pairs={{2,4},{6,8},{10,12},{14,16},{18,20},{22,24},{26,28},{30,32},{34,36... | collective-permute-start | bytes 1769480 | tf_op jit(solution)/shard_map/ppermute | solution.py:280
  25.2 16.4 %collective-permute-start.3 = (f32[384,896]{1,0:T(8,128)S(1)}, f32[384,896]{1,0:T(8,128)S(1)}, u32[]{:S(2)}, u32[]{:S(2)}) collective-permute-start(f32[384,896]{1,0:T(8,128)S(1)} %get-tuple-element.22), channel_id=1, source_target_pairs={{0,2},{4,6},{8,10},{12,14},{16,18},{20,22},{24,26},{28,30},{32,34}... | collective-permute-start | bytes 4128776 | tf_op jit(solution)/shard_map/ppermute | solution.py:280
  26.5 15.1 %collective-permute-start.2 = (f32[384,512]{1,0:T(8,128)S(1)}, f32[384,512]{1,0:T(8,128)S(1)}, u32[]{:S(2)}, u32[]{:S(2)}) collective-permute-start(f32[384,512]{1,0:T(8,128)S(1)} %get-tuple-element.21.pay), channel_id=1, source_target_pairs={{2,6},{10,14},{18,22},{26,30},{34,38},{42,46},{50,54},{58,62},{66,... | collective-permute-start | bytes 2359304 | tf_op jit(solution)/shard_map/ppermute | solution.py:280
  46.5 16.4 %collective-permute-start.4 = (f32[384,512]{1,0:T(8,128)S(1)}, f32[384,512]{1,0:T(8,128)S(1)}, u32[]{:S(2)}, u32[]{:S(2)}) collective-permute-start(f32[384,512]{1,0:T(8,128)S(1)} %get-tuple-element.25.pay), channel_id=1, source_target_pairs={{10,6},{18,14},{26,22},{34,30},{42,38},{50,46},{58,54},{66,62},{74... | collective-permute-start | bytes 2359304 | tf_op jit(solution)/shard_map/ppermute | solution.py:280
where the time goes:
time: 63.4 us; the launch traced here: 63.2 us
  waiting for transfers between devices  24.1 us (38%)
  starting transfers between devices  20.9 us (33%)
  Pallas kernels  17 us (27%)
  between operations  0.92 us (1%)
    ppermute x5, waiting for transfers between devices, send(): lax.ppermute(block, 'layer', [(i % size, j % size) for i, j in route])  24.1 us
    ppermute x5, starting transfers between devices, send(): lax.ppermute(block, 'layer', [(i % size, j % size) for i, j in route])  20.9 us
    pallas_call x1, Pallas kernels, reduce_chain(): call(first_kernel, (like(2, N, W), *outputs), (vmem(), in_hbm(), in_hbm()...  5.21 us
    pallas_call x1, Pallas kernels, reduce_chain(): call(fourth_kernel, (like(N, N + C), *outputs), (vmem(), in_hbm(), in_hbm...  4.89 us
    pallas_call x1, Pallas kernels, reduce_chain(): call(second_kernel, (like(N, N), like(N, N), like(N, C)), (vmem(), vmem()...  4.7 us
    pallas_call x1, Pallas kernels, reduce_chain(): call(third_kernel, (like(N, N + C), like(N, W), *outputs), (vmem(), vmem(...  2.19 us
  transfers between devices with their start and end apart: 5, of which 4 were waited for; matrix products, arithmetic and copies ran while one was open for 0% of the time, Pallas kernels for 7%

commit v1 on v0

v1 whole, which is shorter than its diff:
```python
import jax
import jax.numpy as jnp
from jax import lax
from jax.experimental import pallas as pl
from jax.experimental.pallas import tpu as pltpu
from jax.sharding import PartitionSpec as P


F32 = jnp.float32
BF16 = jnp.bfloat16
N = 384
C = 128
W = 2 * N + C
MIB = 1 << 20


def eye():
    rows = lax.broadcasted_iota(jnp.int32, (N, N), 0)
    return rows == lax.broadcasted_iota(jnp.int32, (N, N), 1)


def halves(x):
    high = x.astype(BF16)
    return high, (x - high.astype(F32)).astype(BF16)


def put_left(ref, x):
    high, low = halves(x)
    ref[:, 0:N] = high
    ref[:, N : 2 * N] = high
    ref[:, 2 * N : 3 * N] = low


def put_right(ref, x, at=0):
    high, low = halves(x)
    cols = slice(at, at + x.shape[1])
    ref[0:N, cols] = high
    ref[N : 2 * N, cols] = low
    ref[2 * N : 3 * N, cols] = high


def put_right_t(ref, x):
    high, low = halves(x)
    ref[:, 0:N] = high
    ref[:, N : 2 * N] = low
    ref[:, 2 * N : 3 * N] = high


def dot(left, right):
    return jnp.dot(left, right, preferred_element_type=F32)


def dot_t(left, right):
    return lax.dot_general(
        left, right, (((1,), (1,)), ((), ())), preferred_element_type=F32
    )


def invert(block, out, left_e, left_p, right_e, right_p, s_e, s_2):
    scale = N / jnp.sum(jnp.where(eye(), block[...], 0.0))
    s_e[...] = jnp.where(eye(), 1.0, 0.0) - scale * block[...]
    put_left(left_e, s_e[...])
    put_right(right_e, s_e[...])
    s_2[...] = dot(left_e[...], right_e[...])
    put_left(left_p, s_2[...])
    put_right(right_p, s_2[...])
    put_right(right_e, dot(left_p[...], right_p[...]))
    cube = dot(left_e[...], right_p[...])
    s_e[...] = jnp.where(eye(), 1.0, 0.0) + s_e[...] + s_2[...] + cube
    put_left(left_p, s_e[...])
    out[...] = scale * (s_e[...] + dot(left_p[...], right_e[...]))


INVERT_SCRATCH = [
    pltpu.VMEM((N, 3 * N), BF16),
    pltpu.VMEM((N, 3 * N), BF16),
    pltpu.VMEM((3 * N, N), BF16),
    pltpu.VMEM((3 * N, N), BF16),
    pltpu.VMEM((N, N), F32),
    pltpu.VMEM((N, N), F32),
]


def pack(out, x):
    out[0:C, :] = x[0:C, :]
    out[C : 2 * C, 0 : 2 * C] = x[C : 2 * C, C:N]
    out[C : 2 * C, 2 * C : N] = x[2 * C : N, 2 * C : N]


def unpack(out, packed):
    out[0:C, :] = packed[0:C, :]
    out[C : 2 * C, C:N] = packed[C : 2 * C, 0 : 2 * C]
    out[2 * C : N, 2 * C : N] = packed[C : 2 * C, 2 * C : N]
    out[C : 2 * C, 0:C] = packed[0:C, C : 2 * C].T
    out[2 * C : N, 0:C] = packed[0:C, 2 * C : N].T
    out[2 * C : N, C : 2 * C] = packed[C : 2 * C, C : 2 * C].T


def pack_rhs(out, x):
    for i in range(3):
        out[2 * C : N, i * C : (i + 1) * C] = x[i * C : (i + 1) * C, :]


def unpack_rhs(packed):
    return jnp.concatenate([packed[2 * C : N, i * C : (i + 1) * C] for i in range(3)], axis=0)


def first_kernel(
    diag, coup, rhs, pay, keep, u_high, inv_out, rhs_out, d_in, u_in, r_in, x_s, right, left, *rest
):
    inv_scratch, sems = rest[:6], rest[6]
    at_low = (lax.axis_index("layer") % 2) == 0
    loads = [
        pltpu.make_async_copy(diag.at[0], d_in.at[0], sems.at[0]),
        pltpu.make_async_copy(coup.at[0], u_in, sems.at[1]),
        pltpu.make_async_copy(rhs.at[0], r_in.at[0], sems.at[2]),
        pltpu.make_async_copy(diag.at[1], d_in.at[1], sems.at[3]),
        pltpu.make_async_copy(coup.at[1], u_high, sems.at[4]),
        pltpu.make_async_copy(rhs.at[1], r_in.at[1], sems.at[5]),
    ]
    for load in loads:
        load.start()
    loads[0].wait()
    invert(d_in.at[0], x_s, *inv_scratch)
    for load in loads[1:]:
        load.wait()
    stores = [
        pltpu.make_async_copy(x_s, inv_out.at[0], sems.at[0]),
        pltpu.make_async_copy(r_in.at[0], rhs_out.at[0], sems.at[1]),
    ]
    for store in stores:
        store.start()

    def finish(of_x, of_d):
        of_x[:, 0:N] = x_s[...]
        put_left(left, x_s[...])
        put_right(right, u_in[...], 0)
        put_right(right, r_in[0], N)
        of_x[:, N:W] = dot(left[...], right[...])
        put_left(left, u_in[...].T)
        put_right(right, of_x[:, N:W])
        of_d[:, 0:N] = d_in[1] - dot(left[...], right[:, 0:N])
        of_d[:, N : 2 * N] = u_high[...]
        of_d[:, 2 * N : W] = r_in[1] - dot(left[...], right[:, N : N + C])

    @pl.when(at_low)
    def _():
        finish(keep, pay)

    @pl.when(jnp.logical_not(at_low))
    def _():
        finish(pay, keep)

    for store in stores:
        store.wait()


def second_kernel(pay, recv, x_b, u_b, r_b, left, right, right_t, d_s, tmp, *inv_scratch):
    at_low = (lax.axis_index("layer") % 2) == 0
    u_s = jnp.where(at_low, pay[:, N : 2 * N], recv[:, N : 2 * N])
    put_left(left, u_s)
    put_right_t(right_t, u_s)
    put_right(right, jnp.where(at_low, recv[...], pay[...]))
    tmp[...] = dot(left[...], right[...])
    put_left(left, tmp[:, 0:N])
    d_old = jnp.where(at_low, pay[:, 0:N], recv[:, 0:N])
    d_s[...] = d_old - dot_t(left[...], right_t[...])
    u_b[...] = -tmp[:, N : 2 * N]
    r_b[...] = jnp.where(at_low, pay[:, 2 * N : W], recv[:, 2 * N : W]) - tmp[:, 2 * N : W]
    invert(d_s, x_b, *inv_scratch)


def third_kernel(keep, x_b, u_b, r_b, packed, whole, thin, t_left, left, right, right_t, w_s):
    at_low = (lax.axis_index("layer") % 2) == 0

    @pl.when(at_low)
    def _():
        w_s[...] = keep[:, N : 2 * N]

    @pl.when(jnp.logical_not(at_low))
    def _():
        w_s[...] = u_b[...].T

    put_left(left, w_s[...])
    put_right_t(right_t, w_s[...])
    put_right(right, x_b[...])
    put_left(t_left, dot(left[...], right[...]))
    put_right(right, r_b[...])
    sign = jnp.where(at_low, 1.0, -1.0)
    whole[...] = keep[:, 0:N] + sign * dot_t(t_left[...], right_t[...])
    thin[...] = keep[:, 2 * N : W] - dot(t_left[...], right[:, 0:C])
    pack(packed, whole)
    pack_rhs(packed, thin)


def spread_kernel(t_left, u_b, r_b, whole, thin, x_b, inv_in, rhs_in, full, inv_out, rhs_out, right, sems):
    del inv_in, rhs_in

    @pl.when((lax.axis_index("layer") % 2) == 0)
    def _():
        stores = [
            pltpu.make_async_copy(x_b, inv_out.at[1], sems.at[0]),
            pltpu.make_async_copy(r_b, rhs_out.at[1], sems.at[1]),
        ]
        for store in stores:
            store.start()
        put_right(right, u_b[...])
        full[:, N : 2 * N] = dot(t_left[...], right[...])
        full[:, 0:N] = whole[...]
        full[:, 2 * N : W] = thin[...]
        for store in stores:
            store.wait()


def left_kernel(full, u_left, out, left, right, right_t):
    @pl.when((lax.axis_index("layer") % 2) == 1)
    def _():
        put_left(left, u_left[...])
        put_right_t(right_t, u_left[...])
        put_right(right, full[...])
        out[...] = dot(left[...], right[...])
        put_left(left, out[:, 0:N])
        out[:, 0:N] = dot_t(left[...], right_t[...])


def fourth_kernel(whole, packed_in, sums, u_high, packed, x_out, t_left, left, right, right_t, d_s, w_s, *inv_scratch):
    @pl.when(lax.axis_index("layer") % 4 == 1)
    def _():
        unpack(w_s, packed_in)
        put_left(left, u_high[...])
        put_right_t(right_t, u_high[...])
        put_right(right, w_s[...])
        put_left(left, dot(left[...], right[...]))
        d_s[...] = whole[...] - dot_t(left[...], right_t[...])
        invert(d_s, x_out, *inv_scratch)
        put_left(left, sums[:, N : 2 * N])
        put_right_t(right_t, sums[:, N : 2 * N])
        put_right(right, x_out[...])
        put_left(t_left, dot(left[...], right[...]))
        d_s[...] = sums[:, 0:N] + dot_t(t_left[...], right_t[...])
        pack(packed, d_s)


def fifth_kernel(
    t_left, whole, thin, packed_in, sums, u_high, x_in, inv_in, rhs_in,
    whole_out, thin_out, inv_out, rhs_out,
    left, right, right_t, d_s, x_s, w_s, r_s, *rest
):
    del inv_in, rhs_in
    inv_scratch, sems = rest[:6], rest[6]
    place = lax.axis_index("layer") % 4

    @pl.when(place == 1)
    def _():
        stores = [
            pltpu.make_async_copy(x_in, inv_out.at[1], sems.at[0]),
            pltpu.make_async_copy(r_s, rhs_out.at[1], sems.at[1]),
        ]
        stores[0].start()
        put_left(left, u_high[...])
        put_right(right, unpack_rhs(packed_in))
        r_s[...] = thin[...] - dot(left[...], right[:, 0:C])
        stores[1].start()
        put_right(right, r_s[...])
        thin_out[...] = sums[:, 2 * N : W] + dot(t_left[...], right[:, 0:C])
        for store in stores:
            store.wait()

    @pl.when(place == 3)
    def _():
        unpack(d_s, packed_in)
        d_s[...] = d_s[...] - sums[:, 0:N]
        invert(d_s, x_s, *inv_scratch)
        w_s[...] = sums[:, N : 2 * N].T
        put_left(left, w_s[...])
        put_right_t(right_t, w_s[...])
        put_right(right, x_s[...])
        put_left(left, dot(left[...], right[...]))
        whole_out[...] = whole[...] - dot_t(left[...], right_t[...])
        put_right(right, unpack_rhs(packed_in) - sums[:, 2 * N : W])
        thin_out[...] = thin[...] - dot(left[...], right[:, 0:C])


def sixth_kernel(whole, packed_in, x_out, d_s, *inv_scratch):
    @pl.when(lax.axis_index("layer") % 4 == 3)
    def _():
        unpack(d_s, packed_in)
        d_s[...] = whole[...] - d_s[...]
        invert(d_s, x_out, *inv_scratch)


def last_kernel(x_in, thin, thin_in, inv_in, rhs_in, inv_out, rhs_out, r_s, sems):
    del inv_in, rhs_in

    @pl.when(lax.axis_index("layer") % 4 == 3)
    def _():
        inv_store = pltpu.make_async_copy(x_in, inv_out.at[1], sems.at[0])
        inv_store.start()
        r_s[...] = thin[...] - thin_in[...]
        rhs_store = pltpu.make_async_copy(r_s, rhs_out.at[1], sems.at[1])
        rhs_store.start()
        inv_store.wait()
        rhs_store.wait()


def vmem():
    return pl.BlockSpec(memory_space=pltpu.VMEM)


def in_hbm():
    return pl.BlockSpec(memory_space=pltpu.HBM)


def like(*shape):
    return jax.ShapeDtypeStruct(shape, F32)


def call(kernel, outs, out_specs, in_specs, scratch, products, aliases=None):
    return pl.pallas_call(
        kernel,
        out_shape=outs,
        in_specs=in_specs,
        out_specs=out_specs,
        scratch_shapes=scratch,
        input_output_aliases=aliases or {},
        compiler_params=pltpu.CompilerParams(vmem_limit_bytes=28 * MIB),
        cost_estimate=pl.CostEstimate(
            flops=int(products * 6 * N * N * N), bytes_accessed=4 * MIB, transcendentals=0
        ),
    )


def reduce_chain(diag_block, coupling, right_side):
    size = lax.axis_size("layer")
    groups = range(size // 4)

    def send(block, route):
        return lax.ppermute(block, "layer", [(i % size, j % size) for i, j in route])

    wide = pltpu.VMEM((3 * N, W), BF16)
    mid = pltpu.VMEM((3 * N, N + C), BF16)
    tall = pltpu.VMEM((3 * N, N), BF16)
    flat = pltpu.VMEM((N, 3 * N), BF16)
    tile = pltpu.VMEM((N, N), F32)
    strip = pltpu.VMEM((N, C), F32)
    sems = pltpu.SemaphoreType.DMA((6,))
    outputs = (like(2, N, N), like(2, N, C))
    half_form = jax.ShapeDtypeStruct((N, 3 * N), BF16)
    triangle = like(2 * C, N)

    pay, keep, u_high, inv_out, rhs_out = call(
        first_kernel,
        (like(N, W), like(N, W), like(N, N), *outputs),
        (vmem(), vmem(), vmem(), in_hbm(), in_hbm()),
        [in_hbm()] * 3,
        [pltpu.VMEM((2, N, N), F32), tile, pltpu.VMEM((2, N, C), F32), tile, mid, flat, *INVERT_SCRATCH, sems],
        6.67,
    )(*[pltpu.with_memory_space_constraint(x, pltpu.HBM) for x in (diag_block, coupling, right_side)])
    recv = send(pay, [(i, i ^ 1) for i in range(size)])
    u_left = send(u_high, [(i, i + 2) for i in range(1, size, 2)])
    x_b, u_b, r_b = call(
        second_kernel,
        (like(N, N), like(N, N), like(N, C)),
        (vmem(), vmem(), vmem()),
        [vmem()] * 2,
        [flat, wide, flat, tile, pltpu.VMEM((N, W), F32), *INVERT_SCRATCH],
        7.33,
    )(pay, recv)
    packed, whole, thin, t_left = call(
        third_kernel,
        (like(N, N), like(N, N), like(N, C), half_form),
        (vmem(),) * 4,
        [vmem()] * 4,
        [flat, tall, flat, tile],
        2.33,
    )(keep, x_b, u_b, r_b)
    packed_in = send(
        packed, [(4 * g + 1, 4 * g + 3) for g in groups] + [(4 * g + 2, 4 * g + 1) for g in groups]
    )
    full, inv_out, rhs_out = call(
        spread_kernel,
        (like(N, W), *outputs),
        (vmem(), in_hbm(), in_hbm()),
        [vmem()] * 6 + [in_hbm()] * 2,
        [tall, sems],
        1,
        {6: 1, 7: 2},
    )(t_left, u_b, r_b, whole, thin, x_b, inv_out, rhs_out)
    full_in = send(full, [(i, i + 1) for i in range(0, size, 2)])
    sums = call(
        left_kernel,
        like(N, W),
        vmem(),
        [vmem()] * 2,
        [flat, wide, flat],
        3.33,
    )(full_in, u_left)
    packed, x_3, t_left = call(
        fourth_kernel,
        (triangle, like(N, N), half_form),
        (vmem(),) * 3,
        [vmem()] * 4,
        [flat, tall, flat, tile, tile, *INVERT_SCRATCH],
        8,
    )(whole, packed_in, sums, u_high)
    down = [(4 * g + 5, 4 * g + 3) for g in groups]
    last_in = send(packed, down)
    whole, thin, inv_out, rhs_out = call(
        fifth_kernel,
        (like(N, N), like(N, C), *outputs),
        (vmem(), vmem(), in_hbm(), in_hbm()),
        [vmem()] * 7 + [in_hbm()] * 2,
        [flat, tall, flat, tile, tile, tile, strip, *INVERT_SCRATCH, sems],
        6.67,
        {7: 2, 8: 3},
    )(t_left, whole, thin, packed_in, sums, u_high, x_3, inv_out, rhs_out)
    thin_in = send(thin, down)
    x_7 = call(
        sixth_kernel,
        like(N, N),
        vmem(),
        [vmem()] * 2,
        [tile, *INVERT_SCRATCH],
        4,
    )(whole, last_in)
    return call(
        last_kernel,
        outputs,
        (in_hbm(), in_hbm()),
        [vmem()] * 3 + [in_hbm()] * 2,
        [strip, sems],
        0.1,
        {3: 0, 4: 1},
    )(x_7, thin, thin_in, inv_out, rhs_out)


def solution(mesh):
    return jax.shard_map(
        reduce_chain,
        mesh=mesh,
        in_specs=(P("layer", None, None), P("layer", None, None), P("layer", None, "rhs")),
        out_specs=(P("layer", None, None), P("layer", None, "rhs")),
        check_vma=False,
    )
```

time: 63.4 us -> 61.1 us (0.964)
  waiting for transfers between devices: 24.1 us -> 19.1 us
  Pallas kernels: 17 us -> 21.7 us
  starting transfers between devices: 20.9 us -> 19.1 us
    ppermute x5 -> x6, waiting for transfers between devices: 24.1 us -> 19.1 us  [send(): lax.ppermute(block, 'layer', [(i % size, j % size) for i, j in route])]
    pallas_call x4 -> x8, Pallas kernels: 12.3 us -> 17 us  [the longest x1 5.79 us: reduce_chain(): call(first_kernel, (like(N, W), like(N, W), like(N, N), *outputs), (vmem(...]
    ppermute x5 -> x6, starting transfers between devices: 20.9 us -> 19.1 us  [send(): lax.ppermute(block, 'layer', [(i % size, j % size) for i, j in route])]
  transfers between devices with their start and end apart: 5 -> 6, of which waited for: 4 -> 4; matrix products, arithmetic and copies ran while one was open for 0% -> 0% of each run, Pallas kernels for 7% -> 6%
where the time goes in v1:
time: 61.1 us; the launch traced here: 60.9 us
  Pallas kernels  21.7 us (36%)
  starting transfers between devices  19.1 us (31%)
  waiting for transfers between devices  19.1 us (31%)
  between operations  0.91 us (1%)
    ppermute x6, starting transfers between devices, send(): lax.ppermute(block, 'layer', [(i % size, j % size) for i, j in route])  19.1 us
    ppermute x6, waiting for transfers between devices, send(): lax.ppermute(block, 'layer', [(i % size, j % size) for i, j in route])  19.1 us
    pallas_call x1, Pallas kernels, reduce_chain(): call(first_kernel, (like(N, W), like(N, W), like(N, N), *outputs), (vmem(...  5.79 us
    pallas_call x1, Pallas kernels, reduce_chain(): call(fourth_kernel, (triangle, like(N, N), half_form), (vmem(),) * 3, [vm...  5.4 us
    pallas_call x1, Pallas kernels, reduce_chain(): call(second_kernel, (like(N, N), like(N, N), like(N, C)), (vmem(), vmem()...  4.7 us
    pallas_call x1, Pallas kernels, reduce_chain(): call(third_kernel, (like(N, N), like(N, N), like(N, C), half_form), (vmem...  2 us
    pallas_call x1, Pallas kernels, reduce_chain(): call(fifth_kernel, (like(N, N), like(N, C), *outputs), (vmem(), vmem(), i...  1.88 us
    pallas_call x1, Pallas kernels, reduce_chain(): call(left_kernel, like(N, W), vmem(), [vmem()] * 2, [flat, wide, flat], 3...  1.78 us
  transfers between devices with their start and end apart: 6, of which 4 were waited for; matrix products, arithmetic and copies ran while one was open for 0% of the time, Pallas kernels for 6%

profile of v1, /device:TPU:1, one launch (start us, length us, event | category | flops | bytes accessed | tf_op | source)
XLA Modules:
  0.0 60.9 jit_solution(12356931418037941559)
XLA Ops:
  0.6 5.8 %shard_map.50 = (f32[384,896]{1,0:T(8,128)S(1)}, f32[384,896]{1,0:T(8,128)S(1)}, f32[384,384]{1,0:T(8,128)S(1)}, f32[2,384,384]{2,1,0:T(8,128)}, f32[2,384,128]{2,1,0:T(8,128)}) custom-call(f32[2,384,384]{2,1,0:T(8,128)} %diag.1, f32[2,384,384]{2,1,0:T(8,128)} %coup.1, f32[2,384,128]{2,1,0:T(8,128)} %rhs.1), custom_call_target="tpu_custom_call" | custom-call | flops 2266056704 | bytes 4194304 | tf_op jit(solution)/shard_map/pallas_call | solution.py:351
  6.4 8.7 %collective-permute-start = (f32[384,896]{1,0:T(8,128)S(1)}, f32[384,896]{1,0:T(8,128)S(1)}, u32[]{:S(2)}, u32[]{:S(2)}) collective-permute-start(f32[384,896]{1,0:T(8,128)S(1)} %get-tuple-element.25.pay), channel_id=1, source_target_pairs={{0,2},{2,0},{4,6},{6,4},{8,10},{10,8},{12,14},{14,12},{16,18},{18,... | collective-permute-start | bytes 4128776 | tf_op jit(solution)/shard_map/ppermute | solution.py:338
  15.2 2.7 %collective-permute-done.recv = f32[384,896]{1,0:T(8,128)S(1)} collective-permute-done((f32[384,896]{1,0:T(8,128)S(1)}, f32[384,896]{1,0:T(8,128)S(1)}, u32[]{:S(2)}, u32[]{:S(2)}) %collective-permute-start) | collective-permute-done | bytes 1376288 | tf_op jit(solution)/shard_map/ppermute | solution.py:338
  17.9 4.7 %shard_map.51 = (f32[384,384]{1,0:T(8,128)S(1)}, f32[384,384]{1,0:T(8,128)S(1)}, f32[384,128]{1,0:T(8,128)S(1)}) custom-call(f32[384,896]{1,0:T(8,128)S(1)} %get-tuple-element.25.pay, f32[384,896]{1,0:T(8,128)S(1)} %collective-permute-done.recv), custom_call_target="tpu_custom_call" | custom-call | flops 2490284032 | bytes 4194304 | tf_op jit(solution)/shard_map/pallas_call | solution.py:361
  22.6 2.0 %shard_map.52 = (f32[384,384]{1,0:T(8,128)S(1)}, f32[384,384]{1,0:T(8,128)S(1)}, f32[384,128]{1,0:T(8,128)S(1)}, bf16[384,1152]{1,0:T(8,128)(2,1)S(1)}) custom-call(f32[384,896]{1,0:T(8,128)S(1)} %get-tuple-element.24.keep, f32[384,384]{1,0:T(8,128)S(1)} %get-tuple-element.26.x_b, f32[384,384]{1,0:T(8,128)S(1)} %get-tuple-element.27.u_b, ...), custom_call_target="tpu_custom_call" | custom-call | flops 791590976 | bytes 4194304 | tf_op jit(solution)/shard_map/pallas_call | solution.py:369
  24.6 0.1 shard_map.53
  24.7 1.3 %collective-permute-start.2 = (f32[384,896]{1,0:T(8,128)S(1)}, f32[384,896]{1,0:T(8,128)S(1)}, u32[]{:S(2)}, u32[]{:S(2)}) collective-permute-start(f32[384,896]{1,0:T(8,128)S(1)} %get-tuple-element.35), channel_id=1, source_target_pairs={{0,2},{4,6},{8,10},{12,14},{16,18},{20,22},{24,26},{28,30},{32,34}... | collective-permute-start | bytes 4128776 | tf_op jit(solution)/shard_map/ppermute | solution.py:338
  26.0 1.9 %collective-permute-start.3 = (f32[384,384]{1,0:T(8,128)S(1)}, f32[384,384]{1,0:T(8,128)S(1)}, u32[]{:S(2)}, u32[]{:S(2)}) collective-permute-start(f32[384,384]{1,0:T(8,128)S(1)} %get-tuple-element.36.u_high), channel_id=1, source_target_pairs={{2,6},{6,10},{10,14},{14,18},{18,22},{22,26},{26,30},{30,34},{34,3... | collective-permute-start | bytes 1769480 | tf_op jit(solution)/shard_map/ppermute | solution.py:338
  28.0 1.9 %collective-permute-start.1 = (f32[384,384]{1,0:T(8,128)S(1)}, f32[384,384]{1,0:T(8,128)S(1)}, u32[]{:S(2)}, u32[]{:S(2)}) collective-permute-start(f32[384,384]{1,0:T(8,128)S(1)} %get-tuple-element.30), channel_id=1, source_target_pairs={{2,6},{10,14},{18,22},{26,30},{34,38},{42,46},{50,54},{58,62},{66,... | collective-permute-start | bytes 1769480 | tf_op jit(solution)/shard_map/ppermute | solution.py:338
  29.9 12.7 %collective-permute-done.3.u_left = f32[384,384]{1,0:T(8,128)S(1)} collective-permute-done((f32[384,384]{1,0:T(8,128)S(1)}, f32[384,384]{1,0:T(8,128)S(1)}, u32[]{:S(2)}, u32[]{:S(2)}) %collective-permute-start.3) | collective-permute-done | bytes 589856 | tf_op jit(solution)/shard_map/ppermute | solution.py:338
  42.5 0.0 collective-permute-done.2.full
  42.5 1.8 %shard_map.54.sums = f32[384,896]{1,0:T(8,128)S(1)} custom-call(f32[384,896]{1,0:T(8,128)S(1)} %collective-permute-done.2.full, f32[384,384]{1,0:T(8,128)S(1)} %collective-permute-done.3.u_left), custom_call_target="tpu_custom_call" | custom-call | flops 1131329664 | bytes 4194304 | tf_op jit(solution)/shard_map/pallas_call | solution.py:390
  44.3 1.2 %collective-permute-done.1.packed_in = f32[384,384]{1,0:T(8,128)S(1)} collective-permute-done((f32[384,384]{1,0:T(8,128)S(1)}, f32[384,384]{1,0:T(8,128)S(1)}, u32[]{:S(2)}, u32[]{:S(2)}) %collective-permute-start.1) | collective-permute-done | bytes 589856 | tf_op jit(solution)/shard_map/ppermute | solution.py:338
  45.5 5.4 %shard_map.55 = (f32[256,384]{1,0:T(8,128)S(1)}, f32[384,384]{1,0:T(8,128)S(1)}, bf16[384,1152]{1,0:T(8,128)(2,1)S(1)}) custom-call(f32[384,384]{1,0:T(8,128)S(1)} %get-tuple-element.29.whole, f32[384,384]{1,0:T(8,128)S(1)} %collective-permute-done.1.packed_in, f32[384,896]{1,0:T(8,128)S(1)} %shard_map.54.sums, f32[384,384]{1,0:T(8,128)S(1)} %get-tuple-element.36.u_high), custom_call_target="tpu_custom_call" | custom-call | flops 2717908992 | bytes 4194304 | tf_op jit(solution)/shard_map/pallas_call | solution.py:398
  50.9 1.3 %collective-permute-start.4 = (f32[256,384]{1,0:T(8,128)S(1)}, f32[256,384]{1,0:T(8,128)S(1)}, u32[]{:S(2)}, u32[]{:S(2)}) collective-permute-start(f32[256,384]{1,0:T(8,128)S(1)} %get-tuple-element.42), channel_id=1, source_target_pairs={{10,6},{18,14},{26,22},{34,30},{42,38},{50,46},{58,54},{66,62},{74... | collective-permute-start | bytes 1179656 | tf_op jit(solution)/shard_map/ppermute | solution.py:338
  52.2 1.9 %shard_map.56 = (f32[384,384]{1,0:T(8,128)S(1)}, f32[384,128]{1,0:T(8,128)S(1)}, f32[2,384,384]{2,1,0:T(8,128)}, f32[2,384,128]{2,1,0:T(8,128)}) custom-call(bf16[384,1152]{1,0:T(8,128)(2,1)S(1)} %get-tuple-element.37.t_left, f32[384,384]{1,0:T(8,128)S(1)} %get-tuple-element.29.whole, ...), custom_call_target="tpu_custom_call", output_to_operand_aliasing={{2}: (7, {}), {3}: (8, {})} | custom-call | flops 2266056704 | bytes 4194304 | tf_op jit(solution)/shard_map/pallas_call | solution.py:408
  54.1 4.0 %collective-permute-start.5 = (f32[384,128]{1,0:T(8,128)S(1)}, f32[384,128]{1,0:T(8,128)S(1)}, u32[]{:S(2)}, u32[]{:S(2)}) collective-permute-start(f32[384,128]{1,0:T(8,128)S(1)} %get-tuple-element.43.thin), channel_id=1, source_target_pairs={{10,6},{18,14},{26,22},{34,30},{42,38},{50,46},{58,54},{66,62},{74... | collective-permute-start | bytes 589832 | tf_op jit(solution)/shard_map/ppermute | solution.py:338
  58.1 0.0 collective-permute-done.4.packed_in
  58.1 2.5 %collective-permute-done.5.thin_in = f32[384,128]{1,0:T(8,128)S(1)} collective-permute-done((f32[384,128]{1,0:T(8,128)S(1)}, f32[384,128]{1,0:T(8,128)S(1)}, u32[]{:S(2)}, u32[]{:S(2)}) %collective-permute-start.5) | collective-permute-done | bytes 196640 | tf_op jit(solution)/shard_map/ppermute | solution.py:338
  60.6 0.1 shard_map.58
  (1 shorter events, 0.0 us)
Async XLA Ops:
  6.4 11.5 %collective-permute-start = (f32[384,896]{1,0:T(8,128)S(1)}, f32[384,896]{1,0:T(8,128)S(1)}, u32[]{:S(2)}, u32[]{:S(2)}) collective-permute-start(f32[384,896]{1,0:T(8,128)S(1)} %get-tuple-element.25.pay), channel_id=1, source_target_pairs={{0,2},{2,0},{4,6},{6,4},{8,10},{10,8},{12,14},{14,12},{16,18},{18,... | collective-permute-start | bytes 4128776 | tf_op jit(solution)/shard_map/ppermute | solution.py:338
  24.7 17.8 %collective-permute-start.2 = (f32[384,896]{1,0:T(8,128)S(1)}, f32[384,896]{1,0:T(8,128)S(1)}, u32[]{:S(2)}, u32[]{:S(2)}) collective-permute-start(f32[384,896]{1,0:T(8,128)S(1)} %get-tuple-element.35), channel_id=1, source_target_pairs={{0,2},{4,6},{8,10},{12,14},{16,18},{20,22},{24,26},{28,30},{32,34}... | collective-permute-start | bytes 4128776 | tf_op jit(solution)/shard_map/ppermute | solution.py:338
  26.0 16.5 %collective-permute-start.3 = (f32[384,384]{1,0:T(8,128)S(1)}, f32[384,384]{1,0:T(8,128)S(1)}, u32[]{:S(2)}, u32[]{:S(2)}) collective-permute-start(f32[384,384]{1,0:T(8,128)S(1)} %get-tuple-element.36.u_high), channel_id=1, source_target_pairs={{2,6},{6,10},{10,14},{14,18},{18,22},{22,26},{26,30},{30,34},{34,3... | collective-permute-start | bytes 1769480 | tf_op jit(solution)/shard_map/ppermute | solution.py:338
  28.0 17.5 %collective-permute-start.1 = (f32[384,384]{1,0:T(8,128)S(1)}, f32[384,384]{1,0:T(8,128)S(1)}, u32[]{:S(2)}, u32[]{:S(2)}) collective-permute-start(f32[384,384]{1,0:T(8,128)S(1)} %get-tuple-element.30), channel_id=1, source_target_pairs={{2,6},{10,14},{18,22},{26,30},{34,38},{42,46},{50,54},{58,62},{66,... | collective-permute-start | bytes 1769480 | tf_op jit(solution)/shard_map/ppermute | solution.py:338
  50.9 7.2 %collective-permute-start.4 = (f32[256,384]{1,0:T(8,128)S(1)}, f32[256,384]{1,0:T(8,128)S(1)}, u32[]{:S(2)}, u32[]{:S(2)}) collective-permute-start(f32[256,384]{1,0:T(8,128)S(1)} %get-tuple-element.42), channel_id=1, source_target_pairs={{10,6},{18,14},{26,22},{34,30},{42,38},{50,46},{58,54},{66,62},{74... | collective-permute-start | bytes 1179656 | tf_op jit(solution)/shard_map/ppermute | solution.py:338
  54.1 6.5 %collective-permute-start.5 = (f32[384,128]{1,0:T(8,128)S(1)}, f32[384,128]{1,0:T(8,128)S(1)}, u32[]{:S(2)}, u32[]{:S(2)}) collective-permute-start(f32[384,128]{1,0:T(8,128)S(1)} %get-tuple-element.43.thin), channel_id=1, source_target_pairs={{10,6},{18,14},{26,22},{34,30},{42,38},{50,46},{58,54},{66,62},{74... | collective-permute-start | bytes 589832 | tf_op jit(solution)/shard_map/ppermute | solution.py:338

commit v2 on v1

--- a/solution.py
+++ b/solution.py
@@ -170,33 +170,28 @@
     invert(d_s, x_b, *inv_scratch)
 
 
-def third_kernel(keep, x_b, u_b, r_b, packed, whole, thin, t_left, left, right, right_t, w_s):
+def third_kernel(keep, x_b, r_b, packed, whole, thin, t_left, left, right, right_t):
+    @pl.when((lax.axis_index("layer") % 2) == 0)
+    def _():
+        put_left(left, keep[:, N : 2 * N])
+        put_right_t(right_t, keep[:, N : 2 * N])
+        put_right(right, x_b[...])
+        put_left(t_left, dot(left[...], right[...]))
+        put_right(right, r_b[...])
+        thin[...] = keep[:, 2 * N : W] - dot(t_left[...], right[:, 0:C])
+        pack_rhs(packed, thin)
+        whole[...] = keep[:, 0:N] + dot_t(t_left[...], right_t[...])
+        pack(packed, whole)
+
+
+def spread_kernel(
+    t_left, u_b, r_b, keep, s_in, thin_in, x_b, inv_in, rhs_in,
+    full, packed, whole, thin, inv_out, rhs_out, left, right, right_t, w_s, sems
+):
+    del inv_in, rhs_in
     at_low = (lax.axis_index("layer") % 2) == 0
 
     @pl.when(at_low)
-    def _():
-        w_s[...] = keep[:, N : 2 * N]
-
-    @pl.when(jnp.logical_not(at_low))
-    def _():
-        w_s[...] = u_b[...].T
-
-    put_left(left, w_s[...])
-    put_right_t(right_t, w_s[...])
-    put_right(right, x_b[...])
-    put_left(t_left, dot(left[...], right[...]))
-    put_right(right, r_b[...])
-    sign = jnp.where(at_low, 1.0, -1.0)
-    whole[...] = keep[:, 0:N] + sign * dot_t(t_left[...], right_t[...])
-    thin[...] = keep[:, 2 * N : W] - dot(t_left[...], right[:, 0:C])
-    pack(packed, whole)
-    pack_rhs(packed, thin)
-
-
-def spread_kernel(t_left, u_b, r_b, whole, thin, x_b, inv_in, rhs_in, full, inv_out, rhs_out, right, sems):
-    del inv_in, rhs_in
-
-    @pl.when((lax.axis_index("layer") % 2) == 0)
     def _():
         stores = [
             pltpu.make_async_copy(x_b, inv_out.at[1], sems.at[0]),
@@ -206,10 +201,23 @@
             store.start()
         put_right(right, u_b[...])
         full[:, N : 2 * N] = dot(t_left[...], right[...])
-        full[:, 0:N] = whole[...]
-        full[:, 2 * N : W] = thin[...]
+        full[:, 0:N] = s_in[...]
+        full[:, 2 * N : W] = thin_in[...]
         for store in stores:
             store.wait()
+
+    @pl.when(jnp.logical_not(at_low))
+    def _():
+        w_s[...] = u_b[...].T
+        put_left(left, w_s[...])
+        put_right_t(right_t, w_s[...])
+        put_right(right, x_b[...])
+        put_left(left, dot(left[...], right[...]))
+        put_right(right, r_b[...])
+        whole[...] = keep[:, 0:N] - dot_t(left[...], right_t[...])
+        thin[...] = keep[:, 2 * N : W] - dot(left[...], right[:, 0:C])
+        pack(packed, whole)
+        pack_rhs(packed, thin)
 
 
 def left_kernel(full, u_left, out, left, right, right_t):
@@ -223,28 +231,34 @@
         out[:, 0:N] = dot_t(left[...], right_t[...])
 
 
-def fourth_kernel(whole, packed_in, sums, u_high, packed, x_out, t_left, left, right, right_t, d_s, w_s, *inv_scratch):
+def fourth_kernel(
+    whole, thin, packed_in, sums, u_high, packed, thin_out, x_out, r_out, left, right, right_t, d_s, *inv_scratch
+):
     @pl.when(lax.axis_index("layer") % 4 == 1)
     def _():
-        unpack(w_s, packed_in)
         put_left(left, u_high[...])
         put_right_t(right_t, u_high[...])
-        put_right(right, w_s[...])
+        put_right(right, unpack_rhs(packed_in))
+        r_out[...] = thin[...] - dot(left[...], right[:, 0:C])
+        unpack(d_s, packed_in)
+        put_right(right, d_s[...])
         put_left(left, dot(left[...], right[...]))
         d_s[...] = whole[...] - dot_t(left[...], right_t[...])
         invert(d_s, x_out, *inv_scratch)
         put_left(left, sums[:, N : 2 * N])
         put_right_t(right_t, sums[:, N : 2 * N])
         put_right(right, x_out[...])
-        put_left(t_left, dot(left[...], right[...]))
-        d_s[...] = sums[:, 0:N] + dot_t(t_left[...], right_t[...])
+        put_left(left, dot(left[...], right[...]))
+        put_right(right, r_out[...])
+        d_s[...] = sums[:, 0:N] + dot_t(left[...], right_t[...])
+        thin_out[...] = sums[:, 2 * N : W] + dot(left[...], right[:, 0:C])
         pack(packed, d_s)
 
 
 def fifth_kernel(
-    t_left, whole, thin, packed_in, sums, u_high, x_in, inv_in, rhs_in,
+    whole, thin, packed_in, sums, x_in, r_in, inv_in, rhs_in,
     whole_out, thin_out, inv_out, rhs_out,
-    left, right, right_t, d_s, x_s, w_s, r_s, *rest
+    left, right, right_t, d_s, x_s, w_s, *rest
 ):
     del inv_in, rhs_in
     inv_scratch, sems = rest[:6], rest[6]
@@ -254,15 +268,10 @@
     def _():
         stores = [
             pltpu.make_async_copy(x_in, inv_out.at[1], sems.at[0]),
-            pltpu.make_async_copy(r_s, rhs_out.at[1], sems.at[1]),
+            pltpu.make_async_copy(r_in, rhs_out.at[1], sems.at[1]),
         ]
-        stores[0].start()
-        put_left(left, u_high[...])
-        put_right(right, unpack_rhs(packed_in))
-        r_s[...] = thin[...] - dot(left[...], right[:, 0:C])
-        stores[1].start()
-        put_right(right, r_s[...])
-        thin_out[...] = sums[:, 2 * N : W] + dot(t_left[...], right[:, 0:C])
+        for store in stores:
+            store.start()
         for store in stores:
             store.wait()
 
@@ -370,23 +379,22 @@
         third_kernel,
         (like(N, N), like(N, N), like(N, C), half_form),
         (vmem(),) * 4,
-        [vmem()] * 4,
-        [flat, tall, flat, tile],
+        [vmem()] * 3,
+        [flat, tall, flat],
         2.33,
-    )(keep, x_b, u_b, r_b)
-    packed_in = send(
-        packed, [(4 * g + 1, 4 * g + 3) for g in groups] + [(4 * g + 2, 4 * g + 1) for g in groups]
-    )
-    full, inv_out, rhs_out = call(
+    )(keep, x_b, r_b)
+    urgent_in = send(packed, [(4 * g + 2, 4 * g + 1) for g in groups])
+    full, packed, whole, thin, inv_out, rhs_out = call(
         spread_kernel,
-        (like(N, W), *outputs),
-        (vmem(), in_hbm(), in_hbm()),
-        [vmem()] * 6 + [in_hbm()] * 2,
-        [tall, sems],
-        1,
-        {6: 1, 7: 2},
-    )(t_left, u_b, r_b, whole, thin, x_b, inv_out, rhs_out)
+        (like(N, W), like(N, N), like(N, N), like(N, C), *outputs),
+        (vmem(), vmem(), vmem(), vmem(), in_hbm(), in_hbm()),
+        [vmem()] * 7 + [in_hbm()] * 2,
+        [flat, tall, flat, tile, sems],
+        2,
+        {7: 4, 8: 5},
+    )(t_left, u_b, r_b, keep, whole, thin, x_b, inv_out, rhs_out)
     full_in = send(full, [(i, i + 1) for i in range(0, size, 2)])
+    packed_in = send(packed, [(4 * g + 1, 4 * g + 3) for g in groups])
     sums = call(
         left_kernel,
         like(N, W),
@@ -395,26 +403,26 @@
         [flat, wide, flat],
         3.33,
     )(full_in, u_left)
-    packed, x_3, t_left = call(
+    packed, down_thin, x_3, r_3 = call(
         fourth_kernel,
-        (triangle, like(N, N), half_form),
-        (vmem(),) * 3,
-        [vmem()] * 4,
-        [flat, tall, flat, tile, tile, *INVERT_SCRATCH],
-        8,
-    )(whole, packed_in, sums, u_high)
+        (triangle, like(N, C), like(N, N), like(N, C)),
+        (vmem(),) * 4,
+        [vmem()] * 5,
+        [flat, tall, flat, tile, *INVERT_SCRATCH],
+        8.67,
+    )(whole, thin, urgent_in, sums, u_high)
     down = [(4 * g + 5, 4 * g + 3) for g in groups]
     last_in = send(packed, down)
+    thin_in = send(down_thin, down)
     whole, thin, inv_out, rhs_out = call(
         fifth_kernel,
         (like(N, N), like(N, C), *outputs),
         (vmem(), vmem(), in_hbm(), in_hbm()),
-        [vmem()] * 7 + [in_hbm()] * 2,
-        [flat, tall, flat, tile, tile, tile, strip, *INVERT_SCRATCH, sems],
+        [vmem()] * 6 + [in_hbm()] * 2,
+        [flat, tall, flat, tile, tile, tile, *INVERT_SCRATCH, sems],
         6.67,
-        {7: 2, 8: 3},
-    )(t_left, whole, thin, packed_in, sums, u_high, x_3, inv_out, rhs_out)
-    thin_in = send(thin, down)
+        {6: 2, 7: 3},
+    )(whole, thin, packed_in, sums, x_3, r_3, inv_out, rhs_out)
     x_7 = call(
         sixth_kernel,
         like(N, N),

time: 61.1 us -> 60 us (0.982)
  starting transfers between devices: 19.1 us -> 17.2 us
  waiting for transfers between devices: 19.1 us -> 20.4 us
    pallas_call x2, Pallas kernels: 5.48 us -> 8.06 us  [the longest x1 6.05 us: reduce_chain(): call(fourth_kernel, (triangle, like(N, C), like(N, N), like(N, C)), (vmem...]
    pallas_call x1, Pallas kernels: 2 us -> 0.02 us  [reduce_chain(): call(third_kernel, (like(N, N), like(N, N), like(N, C), half_form), (vmem...]
    ppermute x6 -> x7, starting transfers between devices: 19.1 us -> 17.2 us  [send(): lax.ppermute(block, 'layer', [(i % size, j % size) for i, j in route])]
    ppermute x6 -> x7, waiting for transfers between devices: 19.1 us -> 20.4 us  [send(): lax.ppermute(block, 'layer', [(i % size, j % size) for i, j in route])]
    pallas_call x1, Pallas kernels: 1.88 us -> 0.94 us  [reduce_chain(): call(fifth_kernel, (like(N, N), like(N, C), *outputs), (vmem(), vmem(), i...]
  transfers between devices with their start and end apart: 6 -> 7, of which waited for: 4 -> 5; matrix products, arithmetic and copies ran while one was open for 0% -> 0% of each run, Pallas kernels for 6% -> 15%
where the time goes in v2:
time: 60 us; the launch traced here: 59.8 us
  Pallas kernels  21.3 us (36%)
  waiting for transfers between devices  20.4 us (34%)
  starting transfers between devices  17.2 us (29%)
  between operations  0.91 us (2%)
    ppermute x7, waiting for transfers between devices, send(): lax.ppermute(block, 'layer', [(i % size, j % size) for i, j in route])  20.4 us
    ppermute x7, starting transfers between devices, send(): lax.ppermute(block, 'layer', [(i % size, j % size) for i, j in route])  17.2 us
    pallas_call x1, Pallas kernels, reduce_chain(): call(fourth_kernel, (triangle, like(N, C), like(N, N), like(N, C)), (vmem...  6.05 us
    pallas_call x1, Pallas kernels, reduce_chain(): call(first_kernel, (like(N, W), like(N, W), like(N, N), *outputs), (vmem(...  5.79 us
    pallas_call x1, Pallas kernels, reduce_chain(): call(second_kernel, (like(N, N), like(N, N), like(N, C)), (vmem(), vmem()...  4.7 us
    pallas_call x1, Pallas kernels, reduce_chain(): call(spread_kernel, (like(N, W), like(N, N), like(N, N), like(N, C), *out...  2.01 us
    pallas_call x1, Pallas kernels, reduce_chain(): call(left_kernel, like(N, W), vmem(), [vmem()] * 2, [flat, wide, flat], 3...  1.77 us
  transfers between devices with their start and end apart: 7, of which 5 were waited for; matrix products, arithmetic and copies ran while one was open for 0% of the time, Pallas kernels for 15%

profile of v2, /device:TPU:1, one launch (start us, length us, event | category | flops | bytes accessed | tf_op | source)
XLA Modules:
  0.0 59.8 jit_solution(9680675406329241843)
XLA Ops:
  0.6 5.8 %shard_map.50 = (f32[384,896]{1,0:T(8,128)S(1)}, f32[384,896]{1,0:T(8,128)S(1)}, f32[384,384]{1,0:T(8,128)S(1)}, f32[2,384,384]{2,1,0:T(8,128)}, f32[2,384,128]{2,1,0:T(8,128)}) custom-call(f32[2,384,384]{2,1,0:T(8,128)} %diag.1, f32[2,384,384]{2,1,0:T(8,128)} %coup.1, f32[2,384,128]{2,1,0:T(8,128)} %rhs.1), custom_call_target="tpu_custom_call" | custom-call | flops 2266056704 | bytes 4194304 | tf_op jit(solution)/shard_map/pallas_call | solution.py:360
  6.4 8.7 %collective-permute-start = (f32[384,896]{1,0:T(8,128)S(1)}, f32[384,896]{1,0:T(8,128)S(1)}, u32[]{:S(2)}, u32[]{:S(2)}) collective-permute-start(f32[384,896]{1,0:T(8,128)S(1)} %get-tuple-element.29.pay), channel_id=1, source_target_pairs={{0,2},{2,0},{4,6},{6,4},{8,10},{10,8},{12,14},{14,12},{16,18},{18,... | collective-permute-start | bytes 4128776 | tf_op jit(solution)/shard_map/ppermute | solution.py:347
  15.2 2.7 %collective-permute-done.recv = f32[384,896]{1,0:T(8,128)S(1)} collective-permute-done((f32[384,896]{1,0:T(8,128)S(1)}, f32[384,896]{1,0:T(8,128)S(1)}, u32[]{:S(2)}, u32[]{:S(2)}) %collective-permute-start) | collective-permute-done | bytes 1376288 | tf_op jit(solution)/shard_map/ppermute | solution.py:347
  17.9 4.7 %shard_map.51 = (f32[384,384]{1,0:T(8,128)S(1)}, f32[384,384]{1,0:T(8,128)S(1)}, f32[384,128]{1,0:T(8,128)S(1)}) custom-call(f32[384,896]{1,0:T(8,128)S(1)} %get-tuple-element.29.pay, f32[384,896]{1,0:T(8,128)S(1)} %collective-permute-done.recv), custom_call_target="tpu_custom_call" | custom-call | flops 2490284032 | bytes 4194304 | tf_op jit(solution)/shard_map/pallas_call | solution.py:370
  22.7 2.0 %shard_map.53 = (f32[384,896]{1,0:T(8,128)S(1)}, f32[384,384]{1,0:T(8,128)S(1)}, f32[384,384]{1,0:T(8,128)S(1)}, f32[384,128]{1,0:T(8,128)S(1)}, f32[2,384,384]{2,1,0:T(8,128)}, /*index=5*/f32[2,384,128]{2,1,0:T(8,128)}) custom-call(bf16[384,1152]{1,0:T(8,128)(2,1)S(1)} %get-tuple-element.32.t_left, ...), custom_call_target="tpu_custom_call", output_to_operand_aliasing={{4}: (7, {}), {5}: (8, {})} | custom-call | flops 679477248 | bytes 4194304 | tf_op jit(solution)/shard_map/pallas_call | solution.py:387
  24.7 1.3 %collective-permute-start.2 = (f32[384,896]{1,0:T(8,128)S(1)}, f32[384,896]{1,0:T(8,128)S(1)}, u32[]{:S(2)}, u32[]{:S(2)}) collective-permute-start(f32[384,896]{1,0:T(8,128)S(1)} %get-tuple-element.41), channel_id=1, source_target_pairs={{0,2},{4,6},{8,10},{12,14},{16,18},{20,22},{24,26},{28,30},{32,34}... | collective-permute-start | bytes 4128776 | tf_op jit(solution)/shard_map/ppermute | solution.py:347
  26.0 1.9 %collective-permute-start.3 = (f32[384,384]{1,0:T(8,128)S(1)}, f32[384,384]{1,0:T(8,128)S(1)}, u32[]{:S(2)}, u32[]{:S(2)}) collective-permute-start(f32[384,384]{1,0:T(8,128)S(1)} %get-tuple-element.42.u_high), channel_id=1, source_target_pairs={{2,6},{6,10},{10,14},{14,18},{18,22},{22,26},{26,30},{30,34},{34,3... | collective-permute-start | bytes 1769480 | tf_op jit(solution)/shard_map/ppermute | solution.py:347
  27.9 1.3 %collective-permute-start.4 = (f32[384,384]{1,0:T(8,128)S(1)}, f32[384,384]{1,0:T(8,128)S(1)}, u32[]{:S(2)}, u32[]{:S(2)}) collective-permute-start(f32[384,384]{1,0:T(8,128)S(1)} %get-tuple-element.43), channel_id=1, source_target_pairs={{4,2},{12,10},{20,18},{28,26},{36,34},{44,42},{52,50},{60,58},{68,... | collective-permute-start | bytes 1769480 | tf_op jit(solution)/shard_map/ppermute | solution.py:347
  29.2 1.3 %collective-permute-start.1 = (f32[384,384]{1,0:T(8,128)S(1)}, f32[384,384]{1,0:T(8,128)S(1)}, u32[]{:S(2)}, u32[]{:S(2)}) collective-permute-start(f32[384,384]{1,0:T(8,128)S(1)} %get-tuple-element.40), channel_id=1, source_target_pairs={{2,6},{10,14},{18,22},{26,30},{34,38},{42,46},{50,54},{58,62},{66,... | collective-permute-start | bytes 1769480 | tf_op jit(solution)/shard_map/ppermute | solution.py:347
  30.5 12.0 %collective-permute-done.3.u_left = f32[384,384]{1,0:T(8,128)S(1)} collective-permute-done((f32[384,384]{1,0:T(8,128)S(1)}, f32[384,384]{1,0:T(8,128)S(1)}, u32[]{:S(2)}, u32[]{:S(2)}) %collective-permute-start.3) | collective-permute-done | bytes 589856 | tf_op jit(solution)/shard_map/ppermute | solution.py:347
  42.5 0.0 collective-permute-done.2.full
  42.5 1.8 %shard_map.54.sums = f32[384,896]{1,0:T(8,128)S(1)} custom-call(f32[384,896]{1,0:T(8,128)S(1)} %collective-permute-done.2.full, f32[384,384]{1,0:T(8,128)S(1)} %collective-permute-done.3.u_left), custom_call_target="tpu_custom_call" | custom-call | flops 1131329664 | bytes 4194304 | tf_op jit(solution)/shard_map/pallas_call | solution.py:398
  44.3 1.2 %collective-permute-done.4.packed_in = f32[384,384]{1,0:T(8,128)S(1)} collective-permute-done((f32[384,384]{1,0:T(8,128)S(1)}, f32[384,384]{1,0:T(8,128)S(1)}, u32[]{:S(2)}, u32[]{:S(2)}) %collective-permute-start.4) | collective-permute-done | bytes 589856 | tf_op jit(solution)/shard_map/ppermute | solution.py:347
  45.4 6.1 %shard_map.55 = (f32[256,384]{1,0:T(8,128)S(1)}, f32[384,128]{1,0:T(8,128)S(1)}, f32[384,384]{1,0:T(8,128)S(1)}, f32[384,128]{1,0:T(8,128)S(1)}) custom-call(f32[384,384]{1,0:T(8,128)S(1)} %get-tuple-element.38.whole, f32[384,128]{1,0:T(8,128)S(1)} %get-tuple-element.39.thin, f32[384,384]{1,0:T(8,128)S(1)} %collective-permute-done.4.packed_in, ...), custom_call_target="tpu_custom_call" | custom-call | flops 2945533952 | bytes 4194304 | tf_op jit(solution)/shard_map/pallas_call | solution.py:406
  51.5 1.3 %collective-permute-start.5 = (f32[256,384]{1,0:T(8,128)S(1)}, f32[256,384]{1,0:T(8,128)S(1)}, u32[]{:S(2)}, u32[]{:S(2)}) collective-permute-start(f32[256,384]{1,0:T(8,128)S(1)} %get-tuple-element.49), channel_id=1, source_target_pairs={{10,6},{18,14},{26,22},{34,30},{42,38},{50,46},{58,54},{66,62},{74... | collective-permute-start | bytes 1179656 | tf_op jit(solution)/shard_map/ppermute | solution.py:347
  52.8 1.3 %collective-permute-start.6 = (f32[384,128]{1,0:T(8,128)S(1)}, f32[384,128]{1,0:T(8,128)S(1)}, u32[]{:S(2)}, u32[]{:S(2)}) collective-permute-start(f32[384,128]{1,0:T(8,128)S(1)} %get-tuple-element.51), channel_id=1, source_target_pairs={{10,6},{18,14},{26,22},{34,30},{42,38},{50,46},{58,54},{66,62},{74... | collective-permute-start | bytes 589832 | tf_op jit(solution)/shard_map/ppermute | solution.py:347
  54.1 0.0 collective-permute-done.1.packed_in
  54.1 0.9 %shard_map.56 = (f32[384,384]{1,0:T(8,128)S(1)}, f32[384,128]{1,0:T(8,128)S(1)}, f32[2,384,384]{2,1,0:T(8,128)}, f32[2,384,128]{2,1,0:T(8,128)}) custom-call(f32[384,384]{1,0:T(8,128)S(1)} %get-tuple-element.38.whole, f32[384,128]{1,0:T(8,128)S(1)} %get-tuple-element.39.thin, ...), custom_call_target="tpu_custom_call", output_to_operand_aliasing={{2}: (6, {}), {3}: (7, {})} | custom-call | flops 2266056704 | bytes 4194304 | tf_op jit(solution)/shard_map/pallas_call | solution.py:417
  55.1 2.4 %collective-permute-done.5.packed_in = f32[256,384]{1,0:T(8,128)S(1)} collective-permute-done((f32[256,384]{1,0:T(8,128)S(1)}, f32[256,384]{1,0:T(8,128)S(1)}, u32[]{:S(2)}, u32[]{:S(2)}) %collective-permute-start.5) | collective-permute-done | bytes 393248 | tf_op jit(solution)/shard_map/ppermute | solution.py:347
  57.5 2.1 %collective-permute-done.6.thin_in = f32[384,128]{1,0:T(8,128)S(1)} collective-permute-done((f32[384,128]{1,0:T(8,128)S(1)}, f32[384,128]{1,0:T(8,128)S(1)}, u32[]{:S(2)}, u32[]{:S(2)}) %collective-permute-start.6) | collective-permute-done | bytes 196640 | tf_op jit(solution)/shard_map/ppermute | solution.py:347
  59.6 0.1 shard_map.58
  (2 shorter events, 0.0 us)
Async XLA Ops:
  6.4 11.5 %collective-permute-start = (f32[384,896]{1,0:T(8,128)S(1)}, f32[384,896]{1,0:T(8,128)S(1)}, u32[]{:S(2)}, u32[]{:S(2)}) collective-permute-start(f32[384,896]{1,0:T(8,128)S(1)} %get-tuple-element.29.pay), channel_id=1, source_target_pairs={{0,2},{2,0},{4,6},{6,4},{8,10},{10,8},{12,14},{14,12},{16,18},{18,... | collective-permute-start | bytes 4128776 | tf_op jit(solution)/shard_map/ppermute | solution.py:347
  24.7 17.8 %collective-permute-start.2 = (f32[384,896]{1,0:T(8,128)S(1)}, f32[384,896]{1,0:T(8,128)S(1)}, u32[]{:S(2)}, u32[]{:S(2)}) collective-permute-start(f32[384,896]{1,0:T(8,128)S(1)} %get-tuple-element.41), channel_id=1, source_target_pairs={{0,2},{4,6},{8,10},{12,14},{16,18},{20,22},{24,26},{28,30},{32,34}... | collective-permute-start | bytes 4128776 | tf_op jit(solution)/shard_map/ppermute | solution.py:347
  26.0 16.5 %collective-permute-start.3 = (f32[384,384]{1,0:T(8,128)S(1)}, f32[384,384]{1,0:T(8,128)S(1)}, u32[]{:S(2)}, u32[]{:S(2)}) collective-permute-start(f32[384,384]{1,0:T(8,128)S(1)} %get-tuple-element.42.u_high), channel_id=1, source_target_pairs={{2,6},{6,10},{10,14},{14,18},{18,22},{22,26},{26,30},{30,34},{34,3... | collective-permute-start | bytes 1769480 | tf_op jit(solution)/shard_map/ppermute | solution.py:347
  27.9 17.5 %collective-permute-start.4 = (f32[384,384]{1,0:T(8,128)S(1)}, f32[384,384]{1,0:T(8,128)S(1)}, u32[]{:S(2)}, u32[]{:S(2)}) collective-permute-start(f32[384,384]{1,0:T(8,128)S(1)} %get-tuple-element.43), channel_id=1, source_target_pairs={{4,2},{12,10},{20,18},{28,26},{36,34},{44,42},{52,50},{60,58},{68,... | collective-permute-start | bytes 1769480 | tf_op jit(solution)/shard_map/ppermute | solution.py:347
  29.2 24.9 %collective-permute-start.1 = (f32[384,384]{1,0:T(8,128)S(1)}, f32[384,384]{1,0:T(8,128)S(1)}, u32[]{:S(2)}, u32[]{:S(2)}) collective-permute-start(f32[384,384]{1,0:T(8,128)S(1)} %get-tuple-element.40), channel_id=1, source_target_pairs={{2,6},{10,14},{18,22},{26,30},{34,38},{42,46},{50,54},{58,62},{66,... | collective-permute-start | bytes 1769480 | tf_op jit(solution)/shard_map/ppermute | solution.py:347
  51.5 6.0 %collective-permute-start.5 = (f32[256,384]{1,0:T(8,128)S(1)}, f32[256,384]{1,0:T(8,128)S(1)}, u32[]{:S(2)}, u32[]{:S(2)}) collective-permute-start(f32[256,384]{1,0:T(8,128)S(1)} %get-tuple-element.49), channel_id=1, source_target_pairs={{10,6},{18,14},{26,22},{34,30},{42,38},{50,46},{58,54},{66,62},{74... | collective-permute-start | bytes 1179656 | tf_op jit(solution)/shard_map/ppermute | solution.py:347
  52.8 6.8 %collective-permute-start.6 = (f32[384,128]{1,0:T(8,128)S(1)}, f32[384,128]{1,0:T(8,128)S(1)}, u32[]{:S(2)}, u32[]{:S(2)}) collective-permute-start(f32[384,128]{1,0:T(8,128)S(1)} %get-tuple-element.51), channel_id=1, source_target_pairs={{10,6},{18,14},{26,22},{34,30},{42,38},{50,46},{58,54},{66,62},{74... | collective-permute-start | bytes 589832 | tf_op jit(solution)/shard_map/ppermute | solution.py:347

commit v3 on v2

v3 whole, which is shorter than its diff:
```python
import jax
import jax.numpy as jnp
from jax import lax
from jax.experimental import pallas as pl
from jax.experimental.pallas import tpu as pltpu
from jax.sharding import PartitionSpec as P


F32 = jnp.float32
BF16 = jnp.bfloat16
N = 384
C = 128
W = 2 * N + C
MIB = 1 << 20


def eye():
    rows = lax.broadcasted_iota(jnp.int32, (N, N), 0)
    return rows == lax.broadcasted_iota(jnp.int32, (N, N), 1)


def halves(x):
    high = x.astype(BF16)
    return high, (x - high.astype(F32)).astype(BF16)


def put_left(ref, x):
    high, low = halves(x)
    ref[:, 0:N] = high
    ref[:, N : 2 * N] = high
    ref[:, 2 * N : 3 * N] = low


def put_right(ref, x, at=0):
    high, low = halves(x)
    cols = slice(at, at + x.shape[1])
    ref[0:N, cols] = high
    ref[N : 2 * N, cols] = low
    ref[2 * N : 3 * N, cols] = high


def put_both(ref, x):
    high, low = halves(x)
    ref[:, 0:N] = high
    ref[:, N : 2 * N] = high
    ref[:, 2 * N : 3 * N] = low
    ref[:, 3 * N : 4 * N] = high


def dot(left, right):
    return jnp.dot(left, right, preferred_element_type=F32)


def dot_t(left, right):
    return lax.dot_general(
        left, right, (((1,), (1,)), ((), ())), preferred_element_type=F32
    )


def as_left(ref):
    return ref[:, 0 : 3 * N]


def as_right_t(ref):
    return ref[:, N : 4 * N]


def invert(block, out, left_e, left_p, right_e, right_p, s_e, s_2, beside=None):
    scale = N / jnp.sum(jnp.where(eye(), block[...], 0.0))
    s_e[...] = jnp.where(eye(), 1.0, 0.0) - scale * block[...]
    put_left(left_e, s_e[...])
    put_right(right_e, s_e[...])
    s_2[...] = dot(left_e[...], right_e[...])
    if beside is not None:
        beside()
    put_left(left_p, s_2[...])
    put_right(right_p, s_2[...])
    put_right(right_e, dot(left_p[...], right_p[...]))
    cube = dot(left_e[...], right_p[...])
    s_e[...] = jnp.where(eye(), 1.0, 0.0) + s_e[...] + s_2[...] + cube
    put_left(left_p, s_e[...])
    out[...] = scale * (s_e[...] + dot(left_p[...], right_e[...]))


INVERT_SCRATCH = [
    pltpu.VMEM((N, 3 * N), BF16),
    pltpu.VMEM((N, 3 * N), BF16),
    pltpu.VMEM((3 * N, N), BF16),
    pltpu.VMEM((3 * N, N), BF16),
    pltpu.VMEM((N, N), F32),
    pltpu.VMEM((N, N), F32),
]


def pack(out, x):
    out[0:C, :] = x[0:C, :]
    out[C : 2 * C, 0 : 2 * C] = x[C : 2 * C, C:N]
    out[C : 2 * C, 2 * C : N] = x[2 * C : N, 2 * C : N]


def unpack(out, packed):
    out[0:C, :] = packed[0:C, :]
    out[C : 2 * C, C:N] = packed[C : 2 * C, 0 : 2 * C]
    out[2 * C : N, 2 * C : N] = packed[C : 2 * C, 2 * C : N]
    out[C : 2 * C, 0:C] = packed[0:C, C : 2 * C].T
    out[2 * C : N, 0:C] = packed[0:C, 2 * C : N].T
    out[2 * C : N, C : 2 * C] = packed[C : 2 * C, C : 2 * C].T


def pack_rhs(out, x):
    for i in range(3):
        out[2 * C : N, i * C : (i + 1) * C] = x[i * C : (i + 1) * C, :]


def unpack_rhs(packed):
    return jnp.concatenate([packed[2 * C : N, i * C : (i + 1) * C] for i in range(3)], axis=0)


def first_kernel(
    diag, coup, rhs, pay, keep, u_high, inv_out, rhs_out, d_in, u_in, r_in, right, left, left_u, *rest
):
    inv_scratch, sems = rest[:6], rest[6]
    at_low = (lax.axis_index("layer") % 2) == 0
    loads = [
        pltpu.make_async_copy(diag.at[0], d_in.at[0], sems.at[0]),
        pltpu.make_async_copy(coup.at[0], u_in, sems.at[1]),
        pltpu.make_async_copy(rhs.at[0], r_in.at[0], sems.at[2]),
        pltpu.make_async_copy(diag.at[1], d_in.at[1], sems.at[3]),
        pltpu.make_async_copy(coup.at[1], u_high, sems.at[4]),
        pltpu.make_async_copy(rhs.at[1], r_in.at[1], sems.at[5]),
    ]
    loads[0].start()
    loads[1].start()
    loads[0].wait()
    for load in loads[2:]:
        load.start()
    loads[1].wait()

    def transpose_u():
        put_left(left_u, u_in[...].T)
        put_right(right, u_in[...], 0)

    def finish(of_x, of_d):
        invert(d_in.at[0], of_x.at[:, 0:N], *inv_scratch, beside=transpose_u)
        for load in loads[2:]:
            load.wait()
        stores = [
            pltpu.make_async_copy(of_x.at[:, 0:N], inv_out.at[0], sems.at[0]),
            pltpu.make_async_copy(r_in.at[0], rhs_out.at[0], sems.at[1]),
        ]
        for store in stores:
            store.start()
        put_left(left, of_x[:, 0:N])
        put_right(right, r_in[0], N)
        of_x[:, N:W] = dot(left[...], right[...])
        put_right(right, of_x[:, N:W])
        of_d[:, 0:N] = d_in[1] - dot(left_u[...], right[:, 0:N])
        of_d[:, 2 * N : W] = r_in[1] - dot(left_u[...], right[:, N : N + C])
        for store in stores:
            store.wait()

    @pl.when(at_low)
    def _():
        finish(keep, pay)
        pay[:, N : 2 * N] = u_high[...]

    @pl.when(jnp.logical_not(at_low))
    def _():
        finish(pay, keep)


def by_role(step, pay, recv):
    at_low = (lax.axis_index("layer") % 2) == 0

    @pl.when(at_low)
    def _():
        step(pay, recv)

    @pl.when(jnp.logical_not(at_low))
    def _():
        step(recv, pay)


def second_kernel(pay, recv, x_b, both, left, right, d_s, *inv_scratch):
    def step(of_d, of_x):
        put_both(both, of_d[:, N : 2 * N])
        put_right(right, of_x[:, 0:N])
        put_left(left, dot(as_left(both), right[...]))
        d_s[...] = of_d[:, 0:N] - dot_t(left[...], as_right_t(both))

    by_role(step, pay, recv)
    invert(d_s, x_b, *inv_scratch)


def third_kernel(keep, x_b, packed, whole, t_left, both, right):
    @pl.when((lax.axis_index("layer") % 2) == 0)
    def _():
        put_both(both, keep[:, N : 2 * N])
        put_right(right, x_b[...])
        put_left(t_left, dot(as_left(both), right[...]))
        whole[...] = keep[:, 0:N] + dot_t(t_left[...], as_right_t(both))
        pack(packed, whole)


def spread_kernel(
    t_left, pay, recv, keep, s_in, x_b, inv_in, rhs_in,
    full, packed, whole, thin, inv_out, rhs_out, both, left, right, u_b, r_b, sems
):
    del inv_in, rhs_in
    at_low = (lax.axis_index("layer") % 2) == 0
    stores = [
        pltpu.make_async_copy(x_b, inv_out.at[1], sems.at[0]),
        pltpu.make_async_copy(r_b, rhs_out.at[1], sems.at[1]),
    ]

    def step(of_d, of_x):
        put_left(left, of_d[:, N : 2 * N])
        put_right(right, of_x[:, N:W])
        u_b[...] = -dot(left[...], right[:, 0:N])
        r_b[...] = of_d[:, 2 * N : W] - dot(left[...], right[:, N : N + C])

    by_role(step, pay, recv)

    @pl.when(at_low)
    def _():
        for store in stores:
            store.start()
        put_right(right, u_b[...], 0)
        put_right(right, r_b[...], N)
        full[:, N : 2 * N] = dot(t_left[...], right[:, 0:N])
        thin[...] = keep[:, 2 * N : W] - dot(t_left[...], right[:, N : N + C])
        full[:, 0:N] = s_in[...]
        full[:, 2 * N : W] = thin[...]
        for store in stores:
            store.wait()

    @pl.when(jnp.logical_not(at_low))
    def _():
        put_both(both, u_b[...].T)
        put_right(right, x_b[...], 0)
        put_left(left, dot(as_left(both), right[:, 0:N]))
        put_right(right, r_b[...], N)
        whole[...] = keep[:, 0:N] - dot_t(left[...], as_right_t(both))
        thin[...] = keep[:, 2 * N : W] - dot(left[...], right[:, N : N + C])
        pack(packed, whole)
        pack_rhs(packed, thin)


def fourth_kernel(whole, packed_in, full, u_high, packed, x_out, t_left, both, left, right, d_s, *inv_scratch):
    @pl.when(lax.axis_index("layer") % 4 == 1)
    def _():
        put_both(both, u_high[...])
        unpack(d_s, packed_in)
        put_right(right, d_s[...])
        put_left(left, dot(as_left(both), right[...]))
        d_s[...] = whole[...] - dot_t(left[...], as_right_t(both))
        invert(d_s, x_out, *inv_scratch, beside=lambda: put_both(both, full[:, N : 2 * N]))
        put_right(right, x_out[...])
        put_left(t_left, dot(as_left(both), right[...]))
        d_s[...] = full[:, 0:N] + dot_t(t_left[...], as_right_t(both))
        pack(packed, d_s)


def rest_kernel(t_left, thin, thin_in, full, u_high, thin_out, r_out, left, right):
    @pl.when(lax.axis_index("layer") % 4 == 1)
    def _():
        put_left(left, u_high[...])
        put_right(right, thin_in[...])
        r_out[...] = thin[...] - dot(left[...], right[...])
        put_right(right, r_out[...])
        thin_out[...] = full[:, 2 * N : W] + dot(t_left[...], right[...])


def left_kernel(full, u_left, sums, both, left, right):
    @pl.when(lax.axis_index("layer") % 4 == 3)
    def _():
        put_both(both, u_left[...])
        put_right(right, full[...])
        sums[...] = dot(as_left(both), right[...])
        put_left(left, sums[:, 0:N])
        sums[:, 0:N] = dot_t(left[...], as_right_t(both))


def fifth_kernel(
    whole, thin, packed_in, sums, u_high, x_in, r_in, inv_in, rhs_in,
    whole_out, thin_out, u_both, inv_out, rhs_out,
    both, left, right, d_s, x_s, *rest
):
    del inv_in, rhs_in
    inv_scratch, sems = rest[:6], rest[6]
    place = lax.axis_index("layer") % 4

    @pl.when(place == 1)
    def _():
        stores = [
            pltpu.make_async_copy(x_in, inv_out.at[1], sems.at[0]),
            pltpu.make_async_copy(r_in, rhs_out.at[1], sems.at[1]),
        ]
        for store in stores:
            store.start()
        for store in stores:
            store.wait()

    @pl.when(place == 3)
    def _():
        unpack(d_s, packed_in)
        d_s[...] = d_s[...] - sums[:, 0:N]
        invert(d_s, x_s, *inv_scratch, beside=lambda: put_both(both, sums[:, N : 2 * N].T))
        put_right(right, x_s[...])
        put_left(left, dot(as_left(both), right[...]))
        whole_out[...] = whole[...] - dot_t(left[...], as_right_t(both))
        put_right(right, unpack_rhs(packed_in) - sums[:, 2 * N : W])
        thin_out[...] = thin[...] - dot(left[...], right[:, 0:C])
        put_both(u_both, u_high[...])


def sixth_kernel(whole, packed_in, u_both, x_out, left, right, d_s, *inv_scratch):
    @pl.when(lax.axis_index("layer") % 4 == 3)
    def _():
        unpack(d_s, packed_in)
        put_right(right, d_s[...])
        put_left(left, dot(as_left(u_both), right[...]))
        d_s[...] = whole[...] - dot_t(left[...], as_right_t(u_both))
        invert(d_s, x_out, *inv_scratch)


def last_kernel(x_in, thin, thin_in, u_both, inv_in, rhs_in, inv_out, rhs_out, right, r_s, sems):
    del inv_in, rhs_in

    @pl.when(lax.axis_index("layer") % 4 == 3)
    def _():
        inv_store = pltpu.make_async_copy(x_in, inv_out.at[1], sems.at[0])
        inv_store.start()
        put_right(right, thin_in[...])
        r_s[...] = thin[...] - dot(as_left(u_both), right[...])
        rhs_store = pltpu.make_async_copy(r_s, rhs_out.at[1], sems.at[1])
        rhs_store.start()
        inv_store.wait()
        rhs_store.wait()


def vmem():
    return pl.BlockSpec(memory_space=pltpu.VMEM)


def in_hbm():
    return pl.BlockSpec(memory_space=pltpu.HBM)


def like(*shape):
    return jax.ShapeDtypeStruct(shape, F32)


def call(kernel, outs, out_specs, in_specs, scratch, products, aliases=None):
    return pl.pallas_call(
        kernel,
        out_shape=outs,
        in_specs=in_specs,
        out_specs=out_specs,
        scratch_shapes=scratch,
        input_output_aliases=aliases or {},
        compiler_params=pltpu.CompilerParams(vmem_limit_bytes=28 * MIB),
        cost_estimate=pl.CostEstimate(
            flops=int(products * 6 * N * N * N), bytes_accessed=4 * MIB, transcendentals=0
        ),
    )


def reduce_chain(diag_block, coupling, right_side):
    size = lax.axis_size("layer")
    groups = range(size // 4)

    def send(block, route):
        return lax.ppermute(block, "layer", [(i % size, j % size) for i, j in route])

    def send_crossed(block, route):
        pairs = [(2 * (i % size) + c, 2 * (j % size) + 1 - c) for i, j in route for c in (0, 1)]
        return lax.ppermute(block, ("layer", "rhs"), pairs)

    wide = pltpu.VMEM((3 * N, W), BF16)
    mid = pltpu.VMEM((3 * N, N + C), BF16)
    tall = pltpu.VMEM((3 * N, N), BF16)
    flat = pltpu.VMEM((N, 3 * N), BF16)
    double = pltpu.VMEM((N, 4 * N), BF16)
    tile = pltpu.VMEM((N, N), F32)
    strip = pltpu.VMEM((N, C), F32)
    sems = pltpu.SemaphoreType.DMA((6,))
    outputs = (like(2, N, N), like(2, N, C))
    half_form = jax.ShapeDtypeStruct((N, 3 * N), BF16)
    triangle = like(2 * C, N)

    pay, keep, u_high, inv_out, rhs_out = call(
        first_kernel,
        (like(N, W), like(N, W), like(N, N), *outputs),
        (vmem(), vmem(), vmem(), in_hbm(), in_hbm()),
        [in_hbm()] * 3,
        [pltpu.VMEM((2, N, N), F32), tile, pltpu.VMEM((2, N, C), F32), mid, flat, flat, *INVERT_SCRATCH, sems],
        6.67,
    )(*[pltpu.with_memory_space_constraint(x, pltpu.HBM) for x in (diag_block, coupling, right_side)])
    recv = send(pay, [(i, i ^ 1) for i in range(size)])
    u_left = send(u_high, [(4 * g + 1, 4 * g + 3) for g in groups])
    x_b = call(
        second_kernel,
        like(N, N),
        vmem(),
        [vmem()] * 2,
        [double, flat, tall, tile, *INVERT_SCRATCH],
        6,
    )(pay, recv)
    packed, whole, t_left = call(
        third_kernel,
        (triangle, like(N, N), half_form),
        (vmem(),) * 3,
        [vmem()] * 2,
        [double, tall],
        2,
    )(keep, x_b)
    urgent_in = send_crossed(packed, [(4 * g + 2, 4 * g + 1) for g in groups])
    full, packed, whole, thin, inv_out, rhs_out = call(
        spread_kernel,
        (like(N, W), like(N, N), like(N, N), like(N, C), *outputs),
        (vmem(), vmem(), vmem(), vmem(), in_hbm(), in_hbm()),
        [vmem()] * 6 + [in_hbm()] * 2,
        [double, flat, mid, tile, strip, sems],
        3.33,
        {6: 4, 7: 5},
    )(t_left, pay, recv, keep, whole, x_b, inv_out, rhs_out)
    full_in = send(full, [(4 * g, 4 * g + 1) for g in groups])
    thin_in = send(thin, [(4 * g + 2, 4 * g + 1) for g in groups])
    packed_in = send(packed, [(4 * g + 1, 4 * g + 3) for g in groups])
    packed, x_3, t_left = call(
        fourth_kernel,
        (triangle, like(N, N), half_form),
        (vmem(),) * 3,
        [vmem()] * 4,
        [double, flat, tall, tile, *INVERT_SCRATCH],
        8,
    )(whole, urgent_in, full_in, u_high)
    down = [(4 * g + 5, 4 * g + 3) for g in groups]
    last_in = send_crossed(packed, down)
    down_thin, r_3 = call(
        rest_kernel,
        (like(N, C), like(N, C)),
        (vmem(),) * 2,
        [vmem()] * 5,
        [flat, pltpu.VMEM((3 * N, C), BF16)],
        0.67,
    )(t_left, thin, thin_in, full_in, u_high)
    thin_in = send(down_thin, down)
    sums = call(
        left_kernel,
        like(N, W),
        vmem(),
        [vmem()] * 2,
        [double, flat, wide],
        3.33,
    )(send(full, [(4 * g + 2, 4 * g + 3) for g in groups]), u_left)
    whole, thin, u_both, inv_out, rhs_out = call(
        fifth_kernel,
        (like(N, N), like(N, C), jax.ShapeDtypeStruct((N, 4 * N), BF16), *outputs),
        (vmem(), vmem(), vmem(), in_hbm(), in_hbm()),
        [vmem()] * 7 + [in_hbm()] * 2,
        [double, flat, tall, tile, tile, *INVERT_SCRATCH, sems],
        6.33,
        {7: 3, 8: 4},
    )(whole, thin, packed_in, sums, u_high, x_3, r_3, inv_out, rhs_out)
    x_7 = call(
        sixth_kernel,
        like(N, N),
        vmem(),
        [vmem()] * 3,
        [flat, tall, tile, *INVERT_SCRATCH],
        6,
    )(whole, last_in, u_both)
    return call(
        last_kernel,
        outputs,
        (in_hbm(), in_hbm()),
        [vmem()] * 4 + [in_hbm()] * 2,
        [pltpu.VMEM((3 * N, C), BF16), strip, sems],
        0.33,
        {4: 0, 5: 1},
    )(x_7, thin, thin_in, u_both, inv_out, rhs_out)


def solution(mesh):
    return jax.shard_map(
        reduce_chain,
        mesh=mesh,
        in_specs=(P("layer", None, None), P("layer", None, None), P("layer", None, "rhs")),
        out_specs=(P("layer", None, None), P("layer", None, "rhs")),
        check_vma=False,
    )
```

time: 60 us -> 53.2 us (0.89)
  waiting for transfers between devices: 20.4 us -> 12.2 us
  starting transfers between devices: 17.2 us -> 18.7 us
  Pallas kernels: 21.3 us -> 20.6 us
    ppermute x7, waiting for transfers between devices: 20.4 us -> 4.85 us  [send(): lax.ppermute(block, 'layer', [(i % size, j % size) for i, j in route])]
    ppermute x0 -> x2, waiting for transfers between devices: none -> 7.31 us  [send_crossed(): return lax.ppermute(block, ('layer', 'rhs'), pairs)]
    ppermute x0 -> x2, starting transfers between devices: none -> 2.61 us  [send_crossed(): return lax.ppermute(block, ('layer', 'rhs'), pairs)]
    pallas_call x7 -> x8, Pallas kernels: 13.5 us -> 11.9 us  [the longest x1 5.33 us: reduce_chain(): call(fourth_kernel, (triangle, like(N, N), half_form), (vmem(),) * 3, [vm...]
    ppermute x7, starting transfers between devices: 17.2 us -> 16.1 us  [send(): lax.ppermute(block, 'layer', [(i % size, j % size) for i, j in route])]
    pallas_call x1, Pallas kernels: 2.01 us -> 2.73 us  [reduce_chain(): call(spread_kernel, (like(N, W), like(N, N), like(N, N), like(N, C), *out...]
  transfers between devices with their start and end apart: 7 -> 9, of which waited for: 5 -> 4; matrix products, arithmetic and copies ran while one was open for 0% -> 0% of each run, Pallas kernels for 15% -> 15%
where the time goes in v3:
time: 53.2 us; the launch traced here: 52.4 us
  Pallas kernels  20.6 us (39%)
  starting transfers between devices  18.7 us (35%)
  waiting for transfers between devices  12.2 us (23%)
  between operations  0.99 us (2%)
    ppermute x7, starting transfers between devices, send(): lax.ppermute(block, 'layer', [(i % size, j % size) for i, j in route])  16.1 us
    ppermute x2, waiting for transfers between devices, send_crossed(): return lax.ppermute(block, ('layer', 'rhs'), pairs)  7.31 us
    pallas_call x1, Pallas kernels, reduce_chain(): call(first_kernel, (like(N, W), like(N, W), like(N, N), *outputs), (vmem(...  5.99 us
    pallas_call x1, Pallas kernels, reduce_chain(): call(fourth_kernel, (triangle, like(N, N), half_form), (vmem(),) * 3, [vm...  5.33 us
    ppermute x7, waiting for transfers between devices, send(): lax.ppermute(block, 'layer', [(i % size, j % size) for i, j in route])  4.85 us
    pallas_call x1, Pallas kernels, reduce_chain(): call(second_kernel, like(N, N), vmem(), [vmem()] * 2, [double, flat, tall...  3.96 us
    pallas_call x1, Pallas kernels, reduce_chain(): call(spread_kernel, (like(N, W), like(N, N), like(N, N), like(N, C), *out...  2.73 us
    ppermute x2, starting transfers between devices, send_crossed(): return lax.ppermute(block, ('layer', 'rhs'), pairs)  2.61 us
  transfers between devices with their start and end apart: 9, of which 4 were waited for; matrix products, arithmetic and copies ran while one was open for 0% of the time, Pallas kernels for 15%

profile of v3, /device:TPU:1, one launch (start us, length us, event | category | flops | bytes accessed | tf_op | source)
XLA Modules:
  0.0 52.4 jit_solution(14206218072271179126)
XLA Ops:
  0.6 6.0 %shard_map.50 = (f32[384,896]{1,0:T(8,128)S(1)}, f32[384,896]{1,0:T(8,128)S(1)}, f32[384,384]{1,0:T(8,128)S(1)}, f32[2,384,384]{2,1,0:T(8,128)}, f32[2,384,128]{2,1,0:T(8,128)}) custom-call(f32[2,384,384]{2,1,0:T(8,128)} %diag.1, f32[2,384,384]{2,1,0:T(8,128)} %coup.1, f32[2,384,128]{2,1,0:T(8,128)} %rhs.1), custom_call_target="tpu_custom_call" | custom-call | flops 2266056704 | bytes 4194304 | tf_op jit(solution)/shard_map/pallas_call | solution.py:392
  6.6 8.8 %collective-permute-start = (f32[384,896]{1,0:T(8,128)S(1)}, f32[384,896]{1,0:T(8,128)S(1)}, u32[]{:S(2)}, u32[]{:S(2)}) collective-permute-start(f32[384,896]{1,0:T(8,128)S(1)} %get-tuple-element.27.pay), channel_id=1, source_target_pairs={{0,2},{2,0},{4,6},{6,4},{8,10},{10,8},{12,14},{14,12},{16,18},{18,... | collective-permute-start | bytes 4128776 | tf_op jit(solution)/shard_map/ppermute | solution.py:374
  15.4 2.7 %collective-permute-done.recv = f32[384,896]{1,0:T(8,128)S(1)} collective-permute-done((f32[384,896]{1,0:T(8,128)S(1)}, f32[384,896]{1,0:T(8,128)S(1)}, u32[]{:S(2)}, u32[]{:S(2)}) %collective-permute-start) | collective-permute-done | bytes 1376288 | tf_op jit(solution)/shard_map/ppermute | solution.py:374
  18.1 4.0 %shard_map.51.x_b = f32[384,384]{1,0:T(8,128)S(1)} custom-call(f32[384,896]{1,0:T(8,128)S(1)} %get-tuple-element.27.pay, f32[384,896]{1,0:T(8,128)S(1)} %collective-permute-done.recv), custom_call_target="tpu_custom_call" | custom-call | flops 2038431744 | bytes 4194304 | tf_op jit(solution)/shard_map/pallas_call | solution.py:402
  22.1 0.2 shard_map.52
  22.3 2.7 %shard_map.53 = (f32[384,896]{1,0:T(8,128)S(1)}, f32[384,384]{1,0:T(8,128)S(1)}, f32[384,384]{1,0:T(8,128)S(1)}, f32[384,128]{1,0:T(8,128)S(1)}, f32[2,384,384]{2,1,0:T(8,128)}, /*index=5*/f32[2,384,128]{2,1,0:T(8,128)}) custom-call(bf16[384,1152]{1,0:T(8,128)(2,1)S(1)} %get-tuple-element.28.t_left, ...), custom_call_target="tpu_custom_call", output_to_operand_aliasing={{4}: (6, {}), {5}: (7, {})} | custom-call | flops 1131329664 | bytes 4194304 | tf_op jit(solution)/shard_map/pallas_call | solution.py:419
  25.1 1.3 %collective-permute-start.5 = (f32[384,896]{1,0:T(8,128)S(1)}, f32[384,896]{1,0:T(8,128)S(1)}, u32[]{:S(2)}, u32[]{:S(2)}) collective-permute-start(f32[384,896]{1,0:T(8,128)S(1)} %get-tuple-element.35), channel_id=1, source_target_pairs={{0,2},{8,10},{16,18},{24,26},{32,34},{40,42},{48,50},{56,58},{64,6... | collective-permute-start | bytes 4128776 | tf_op jit(solution)/shard_map/ppermute | solution.py:374
  26.4 0.7 %collective-permute-start.2 = (f32[384,896]{1,0:T(8,128)S(1)}, f32[384,896]{1,0:T(8,128)S(1)}, u32[]{:S(2)}, u32[]{:S(2)}) collective-permute-start(f32[384,896]{1,0:T(8,128)S(1)} %get-tuple-element.35), channel_id=1, source_target_pairs={{4,6},{12,14},{20,22},{28,30},{36,38},{44,46},{52,54},{60,62},{68,... | collective-permute-start | bytes 4128776 | tf_op jit(solution)/shard_map/ppermute | solution.py:374
  27.1 1.3 %collective-permute-start.4 = (f32[256,384]{1,0:T(8,128)S(1)}, f32[256,384]{1,0:T(8,128)S(1)}, u32[]{:S(2)}, u32[]{:S(2)}) collective-permute-start(f32[256,384]{1,0:T(8,128)S(1)} %get-tuple-element.37), channel_id=1, source_target_pairs={{4,3},{5,2},{12,11},{13,10},{20,19},{21,18},{28,27},{29,26},{36,35... | collective-permute-start | bytes 1179656 | tf_op jit(solution)/shard_map/ppermute | solution.py:378
  28.4 1.3 %collective-permute-start.3 = (f32[384,384]{1,0:T(8,128)S(1)}, f32[384,384]{1,0:T(8,128)S(1)}, u32[]{:S(2)}, u32[]{:S(2)}) collective-permute-start(f32[384,384]{1,0:T(8,128)S(1)} %get-tuple-element.36.u_high), channel_id=1, source_target_pairs={{2,6},{10,14},{18,22},{26,30},{34,38},{42,46},{50,54},{58,62},{66,... | collective-permute-start | bytes 1769480 | tf_op jit(solution)/shard_map/ppermute | solution.py:374
  29.8 1.3 %collective-permute-start.1 = (f32[384,384]{1,0:T(8,128)S(1)}, f32[384,384]{1,0:T(8,128)S(1)}, u32[]{:S(2)}, u32[]{:S(2)}) collective-permute-start(f32[384,384]{1,0:T(8,128)S(1)} %get-tuple-element.34), channel_id=1, source_target_pairs={{2,6},{10,14},{18,22},{26,30},{34,38},{42,46},{50,54},{58,62},{66,... | collective-permute-start | bytes 1769480 | tf_op jit(solution)/shard_map/ppermute | solution.py:374
  31.1 6.3 %collective-permute-done.4.packed_in = f32[256,384]{1,0:T(8,128)S(1)} collective-permute-done((f32[256,384]{1,0:T(8,128)S(1)}, f32[256,384]{1,0:T(8,128)S(1)}, u32[]{:S(2)}, u32[]{:S(2)}) %collective-permute-start.4) | collective-permute-done | bytes 393248 | tf_op jit(solution)/shard_map/ppermute | solution.py:378
  37.4 1.3 %collective-permute-start.6 = (f32[384,128]{1,0:T(8,128)S(1)}, f32[384,128]{1,0:T(8,128)S(1)}, u32[]{:S(2)}, u32[]{:S(2)}) collective-permute-start(f32[384,128]{1,0:T(8,128)S(1)} %get-tuple-element.33.thin), channel_id=1, source_target_pairs={{4,2},{12,10},{20,18},{28,26},{36,34},{44,42},{52,50},{60,58},{68,... | collective-permute-start | bytes 589832 | tf_op jit(solution)/shard_map/ppermute | solution.py:374
  38.7 0.0 collective-permute-done.5.full
  38.7 5.3 %shard_map.55 = (f32[256,384]{1,0:T(8,128)S(1)}, f32[384,384]{1,0:T(8,128)S(1)}, bf16[384,1152]{1,0:T(8,128)(2,1)S(1)}) custom-call(f32[384,384]{1,0:T(8,128)S(1)} %get-tuple-element.32.whole, f32[256,384]{1,0:T(8,128)S(1)} %collective-permute-done.4.packed_in, f32[384,896]{1,0:T(8,128)S(1)} %collective-permute-done.5.full, ...), custom_call_target="tpu_custom_call" | custom-call | flops 2717908992 | bytes 4194304 | tf_op jit(solution)/shard_map/pallas_call | solution.py:431
  44.1 1.3 %collective-permute-start.7 = (f32[256,384]{1,0:T(8,128)S(1)}, f32[256,384]{1,0:T(8,128)S(1)}, u32[]{:S(2)}, u32[]{:S(2)}) collective-permute-start(f32[256,384]{1,0:T(8,128)S(1)} %get-tuple-element.44), channel_id=1, source_target_pairs={{10,7},{11,6},{18,15},{19,14},{26,23},{27,22},{34,31},{35,30},{42,... | collective-permute-start | bytes 1179656 | tf_op jit(solution)/shard_map/ppermute | solution.py:378
  45.4 1.1 %shard_map.56 = (f32[384,128]{1,0:T(8,128)S(1)}, f32[384,128]{1,0:T(8,128)S(1)}) custom-call(bf16[384,1152]{1,0:T(8,128)(2,1)S(1)} %get-tuple-element.39.t_left, f32[384,128]{1,0:T(8,128)S(1)} %get-tuple-element.33.thin, f32[384,128]{1,0:T(8,128)S(1)} %collective-permute-done.6.thin_in, f32[384,896]{1,0:T(8,128)S(1)} %collective-permute-done.5.full, ...), custom_call_target="tpu_custom_call" | custom-call | flops 227624880 | bytes 4194304 | tf_op jit(solution)/shard_map/pallas_call | solution.py:441
  46.5 1.3 %collective-permute-start.8 = (f32[384,128]{1,0:T(8,128)S(1)}, f32[384,128]{1,0:T(8,128)S(1)}, u32[]{:S(2)}, u32[]{:S(2)}) collective-permute-start(f32[384,128]{1,0:T(8,128)S(1)} %get-tuple-element.47), channel_id=1, source_target_pairs={{10,6},{18,14},{26,22},{34,30},{42,38},{50,46},{58,54},{66,62},{74... | collective-permute-start | bytes 589832 | tf_op jit(solution)/shard_map/ppermute | solution.py:374
  47.9 0.0 collective-permute-done.2.full
  47.9 0.2 shard_map.54.sums
  48.1 0.9 %shard_map.57 = (f32[384,384]{1,0:T(8,128)S(1)}, f32[384,128]{1,0:T(8,128)S(1)}, bf16[384,1536]{1,0:T(8,128)(2,1)S(1)}, f32[2,384,384]{2,1,0:T(8,128)}, f32[2,384,128]{2,1,0:T(8,128)}) custom-call(f32[384,384]{1,0:T(8,128)S(1)} %get-tuple-element.32.whole, f32[384,128]{1,0:T(8,128)S(1)} %get-tuple-element.33.thin, ...), custom_call_target="tpu_custom_call", output_to_operand_aliasing={{3}: (7, {}), {4}: (8, {})} | custom-call | flops 2150545408 | bytes 4194304 | tf_op jit(solution)/shard_map/pallas_call | solution.py:458
  49.1 1.0 %collective-permute-done.7.packed_in = f32[256,384]{1,0:T(8,128)S(1)} collective-permute-done((f32[256,384]{1,0:T(8,128)S(1)}, f32[256,384]{1,0:T(8,128)S(1)}, u32[]{:S(2)}, u32[]{:S(2)}) %collective-permute-start.7) | collective-permute-done | bytes 393248 | tf_op jit(solution)/shard_map/ppermute | solution.py:378
  50.1 2.1 %collective-permute-done.8.thin_in = f32[384,128]{1,0:T(8,128)S(1)} collective-permute-done((f32[384,128]{1,0:T(8,128)S(1)}, f32[384,128]{1,0:T(8,128)S(1)}, u32[]{:S(2)}, u32[]{:S(2)}) %collective-permute-start.8) | collective-permute-done | bytes 196640 | tf_op jit(solution)/shard_map/ppermute | solution.py:374
  52.2 0.1 shard_map.59
  (4 shorter events, 0.0 us)
Async XLA Ops:
  6.6 11.5 %collective-permute-start = (f32[384,896]{1,0:T(8,128)S(1)}, f32[384,896]{1,0:T(8,128)S(1)}, u32[]{:S(2)}, u32[]{:S(2)}) collective-permute-start(f32[384,896]{1,0:T(8,128)S(1)} %get-tuple-element.27.pay), channel_id=1, source_target_pairs={{0,2},{2,0},{4,6},{6,4},{8,10},{10,8},{12,14},{14,12},{16,18},{18,... | collective-permute-start | bytes 4128776 | tf_op jit(solution)/shard_map/ppermute | solution.py:374
  25.1 13.7 %collective-permute-start.5 = (f32[384,896]{1,0:T(8,128)S(1)}, f32[384,896]{1,0:T(8,128)S(1)}, u32[]{:S(2)}, u32[]{:S(2)}) collective-permute-start(f32[384,896]{1,0:T(8,128)S(1)} %get-tuple-element.35), channel_id=1, source_target_pairs={{0,2},{8,10},{16,18},{24,26},{32,34},{40,42},{48,50},{56,58},{64,6... | collective-permute-start | bytes 4128776 | tf_op jit(solution)/shard_map/ppermute | solution.py:374
  26.4 21.5 %collective-permute-start.2 = (f32[384,896]{1,0:T(8,128)S(1)}, f32[384,896]{1,0:T(8,128)S(1)}, u32[]{:S(2)}, u32[]{:S(2)}) collective-permute-start(f32[384,896]{1,0:T(8,128)S(1)} %get-tuple-element.35), channel_id=1, source_target_pairs={{4,6},{12,14},{20,22},{28,30},{36,38},{44,46},{52,54},{60,62},{68,... | collective-permute-start | bytes 4128776 | tf_op jit(solution)/shard_map/ppermute | solution.py:374
  27.1 10.3 %collective-permute-start.4 = (f32[256,384]{1,0:T(8,128)S(1)}, f32[256,384]{1,0:T(8,128)S(1)}, u32[]{:S(2)}, u32[]{:S(2)}) collective-permute-start(f32[256,384]{1,0:T(8,128)S(1)} %get-tuple-element.37), channel_id=1, source_target_pairs={{4,3},{5,2},{12,11},{13,10},{20,19},{21,18},{28,27},{29,26},{36,35... | collective-permute-start | bytes 1179656 | tf_op jit(solution)/shard_map/ppermute | solution.py:378
  28.4 19.4 %collective-permute-start.3 = (f32[384,384]{1,0:T(8,128)S(1)}, f32[384,384]{1,0:T(8,128)S(1)}, u32[]{:S(2)}, u32[]{:S(2)}) collective-permute-start(f32[384,384]{1,0:T(8,128)S(1)} %get-tuple-element.36.u_high), channel_id=1, source_target_pairs={{2,6},{10,14},{18,22},{26,30},{34,38},{42,46},{50,54},{58,62},{66,... | collective-permute-start | bytes 1769480 | tf_op jit(solution)/shard_map/ppermute | solution.py:374
  29.8 18.4 %collective-permute-start.1 = (f32[384,384]{1,0:T(8,128)S(1)}, f32[384,384]{1,0:T(8,128)S(1)}, u32[]{:S(2)}, u32[]{:S(2)}) collective-permute-start(f32[384,384]{1,0:T(8,128)S(1)} %get-tuple-element.34), channel_id=1, source_target_pairs={{2,6},{10,14},{18,22},{26,30},{34,38},{42,46},{50,54},{58,62},{66,... | collective-permute-start | bytes 1769480 | tf_op jit(solution)/shard_map/ppermute | solution.py:374
  37.4 8.0 %collective-permute-start.6 = (f32[384,128]{1,0:T(8,128)S(1)}, f32[384,128]{1,0:T(8,128)S(1)}, u32[]{:S(2)}, u32[]{:S(2)}) collective-permute-start(f32[384,128]{1,0:T(8,128)S(1)} %get-tuple-element.33.thin), channel_id=1, source_target_pairs={{4,2},{12,10},{20,18},{28,26},{36,34},{44,42},{52,50},{60,58},{68,... | collective-permute-start | bytes 589832 | tf_op jit(solution)/shard_map/ppermute | solution.py:374
  44.1 6.0 %collective-permute-start.7 = (f32[256,384]{1,0:T(8,128)S(1)}, f32[256,384]{1,0:T(8,128)S(1)}, u32[]{:S(2)}, u32[]{:S(2)}) collective-permute-start(f32[256,384]{1,0:T(8,128)S(1)} %get-tuple-element.44), channel_id=1, source_target_pairs={{10,7},{11,6},{18,15},{19,14},{26,23},{27,22},{34,31},{35,30},{42,... | collective-permute-start | bytes 1179656 | tf_op jit(solution)/shard_map/ppermute | solution.py:378
  46.5 5.6 %collective-permute-start.8 = (f32[384,128]{1,0:T(8,128)S(1)}, f32[384,128]{1,0:T(8,128)S(1)}, u32[]{:S(2)}, u32[]{:S(2)}) collective-permute-start(f32[384,128]{1,0:T(8,128)S(1)} %get-tuple-element.47), channel_id=1, source_target_pairs={{10,6},{18,14},{26,22},{34,30},{42,38},{50,46},{58,54},{66,62},{74... | collective-permute-start | bytes 589832 | tf_op jit(solution)/shard_map/ppermute | solution.py:374

commit v4 on v3

--- a/solution.py
+++ b/solution.py
@@ -14,9 +14,18 @@
 MIB = 1 << 20
 
 
-def eye():
-    rows = lax.broadcasted_iota(jnp.int32, (N, N), 0)
-    return rows == lax.broadcasted_iota(jnp.int32, (N, N), 1)
+def unit():
+    rows = lax.broadcasted_iota(jnp.int32, (C, C), 0)
+    return rows == lax.broadcasted_iota(jnp.int32, (C, C), 1)
+
+
+def diagonal_blocks():
+    return [slice(i * C, (i + 1) * C) for i in range(3)]
+
+
+def add_identity(ref):
+    for at in diagonal_blocks():
+        ref[at, at] = ref[at, at] + jnp.where(unit(), 1.0, 0.0)
 
 
 def halves(x):
@@ -66,8 +75,10 @@
 
 
 def invert(block, out, left_e, left_p, right_e, right_p, s_e, s_2, beside=None):
-    scale = N / jnp.sum(jnp.where(eye(), block[...], 0.0))
-    s_e[...] = jnp.where(eye(), 1.0, 0.0) - scale * block[...]
+    kept = sum(jnp.where(unit(), block[at, at], 0.0) for at in diagonal_blocks())
+    scale = N / jnp.sum(jnp.sum(kept, axis=0, keepdims=True), axis=1, keepdims=True)
+    s_e[...] = -(scale * block[...])
+    add_identity(s_e)
     put_left(left_e, s_e[...])
     put_right(right_e, s_e[...])
     s_2[...] = dot(left_e[...], right_e[...])
@@ -77,7 +88,8 @@
     put_right(right_p, s_2[...])
     put_right(right_e, dot(left_p[...], right_p[...]))
     cube = dot(left_e[...], right_p[...])
-    s_e[...] = jnp.where(eye(), 1.0, 0.0) + s_e[...] + s_2[...] + cube
+    s_e[...] = s_e[...] + s_2[...] + cube
+    add_identity(s_e)
     put_left(left_p, s_e[...])
     out[...] = scale * (s_e[...] + dot(left_p[...], right_e[...]))
 
@@ -129,14 +141,12 @@
         pltpu.make_async_copy(coup.at[1], u_high, sems.at[4]),
         pltpu.make_async_copy(rhs.at[1], r_in.at[1], sems.at[5]),
     ]
-    loads[0].start()
-    loads[1].start()
+    for load in loads:
+        load.start()
     loads[0].wait()
-    for load in loads[2:]:
-        load.start()
-    loads[1].wait()
 
     def transpose_u():
+        loads[1].wait()
         put_left(left_u, u_in[...].T)
         put_right(right, u_in[...], 0)
 

time: 53.2 us -> 52.7 us (level)
  transfers between devices with their start and end apart: 9 -> 9, of which waited for: 4 -> 4; matrix products, arithmetic and copies ran while one was open for 0% -> 0% of each run, Pallas kernels for 15% -> 14%
where the time goes in v4:
time: 52.7 us; the launch traced here: 52.1 us
  Pallas kernels  20.3 us (39%)
  starting transfers between devices  18.7 us (35%)
  waiting for transfers between devices  12.2 us (23%)
  between operations  0.99 us (2%)
    ppermute x7, starting transfers between devices, send(): lax.ppermute(block, 'layer', [(i % size, j % size) for i, j in route])  16.1 us
    ppermute x2, waiting for transfers between devices, send_crossed(): return lax.ppermute(block, ('layer', 'rhs'), pairs)  7.31 us
    pallas_call x1, Pallas kernels, reduce_chain(): call(first_kernel, (like(N, W), like(N, W), like(N, N), *outputs), (vmem(...  5.88 us
    pallas_call x1, Pallas kernels, reduce_chain(): call(fourth_kernel, (triangle, like(N, N), half_form), (vmem(),) * 3, [vm...  5.19 us
    ppermute x7, waiting for transfers between devices, send(): lax.ppermute(block, 'layer', [(i % size, j % size) for i, j in route])  4.85 us
    pallas_call x1, Pallas kernels, reduce_chain(): call(second_kernel, like(N, N), vmem(), [vmem()] * 2, [double, flat, tall...  3.86 us
    pallas_call x1, Pallas kernels, reduce_chain(): call(spread_kernel, (like(N, W), like(N, N), like(N, N), like(N, C), *out...  2.74 us
    ppermute x2, starting transfers between devices, send_crossed(): return lax.ppermute(block, ('layer', 'rhs'), pairs)  2.61 us
  transfers between devices with their start and end apart: 9, of which 4 were waited for; matrix products, arithmetic and copies ran while one was open for 0% of the time, Pallas kernels for 14%

profile of v4, /device:TPU:1, one launch (start us, length us, event | category | flops | bytes accessed | tf_op | source)
XLA Modules:
  0.0 52.1 jit_solution(3575388591980666602)
XLA Ops:
  0.6 5.9 %shard_map.50 = (f32[384,896]{1,0:T(8,128)S(1)}, f32[384,896]{1,0:T(8,128)S(1)}, f32[384,384]{1,0:T(8,128)S(1)}, f32[2,384,384]{2,1,0:T(8,128)}, f32[2,384,128]{2,1,0:T(8,128)}) custom-call(f32[2,384,384]{2,1,0:T(8,128)} %diag.1, f32[2,384,384]{2,1,0:T(8,128)} %coup.1, f32[2,384,128]{2,1,0:T(8,128)} %rhs.1), custom_call_target="tpu_custom_call" | custom-call | flops 2266056704 | bytes 4194304 | tf_op jit(solution)/shard_map/pallas_call | solution.py:402
  6.5 8.8 %collective-permute-start = (f32[384,896]{1,0:T(8,128)S(1)}, f32[384,896]{1,0:T(8,128)S(1)}, u32[]{:S(2)}, u32[]{:S(2)}) collective-permute-start(f32[384,896]{1,0:T(8,128)S(1)} %get-tuple-element.27.pay), channel_id=1, source_target_pairs={{0,2},{2,0},{4,6},{6,4},{8,10},{10,8},{12,14},{14,12},{16,18},{18,... | collective-permute-start | bytes 4128776 | tf_op jit(solution)/shard_map/ppermute | solution.py:384
  15.3 2.7 %collective-permute-done.recv = f32[384,896]{1,0:T(8,128)S(1)} collective-permute-done((f32[384,896]{1,0:T(8,128)S(1)}, f32[384,896]{1,0:T(8,128)S(1)}, u32[]{:S(2)}, u32[]{:S(2)}) %collective-permute-start) | collective-permute-done | bytes 1376288 | tf_op jit(solution)/shard_map/ppermute | solution.py:384
  18.0 3.9 %shard_map.51.x_b = f32[384,384]{1,0:T(8,128)S(1)} custom-call(f32[384,896]{1,0:T(8,128)S(1)} %get-tuple-element.27.pay, f32[384,896]{1,0:T(8,128)S(1)} %collective-permute-done.recv), custom_call_target="tpu_custom_call" | custom-call | flops 2038431744 | bytes 4194304 | tf_op jit(solution)/shard_map/pallas_call | solution.py:412
  21.9 0.2 shard_map.52
  22.1 2.7 %shard_map.53 = (f32[384,896]{1,0:T(8,128)S(1)}, f32[384,384]{1,0:T(8,128)S(1)}, f32[384,384]{1,0:T(8,128)S(1)}, f32[384,128]{1,0:T(8,128)S(1)}, f32[2,384,384]{2,1,0:T(8,128)}, /*index=5*/f32[2,384,128]{2,1,0:T(8,128)}) custom-call(bf16[384,1152]{1,0:T(8,128)(2,1)S(1)} %get-tuple-element.28.t_left, ...), custom_call_target="tpu_custom_call", output_to_operand_aliasing={{4}: (6, {}), {5}: (7, {})} | custom-call | flops 1131329664 | bytes 4194304 | tf_op jit(solution)/shard_map/pallas_call | solution.py:429
  24.9 1.3 %collective-permute-start.5 = (f32[384,896]{1,0:T(8,128)S(1)}, f32[384,896]{1,0:T(8,128)S(1)}, u32[]{:S(2)}, u32[]{:S(2)}) collective-permute-start(f32[384,896]{1,0:T(8,128)S(1)} %get-tuple-element.35), channel_id=1, source_target_pairs={{0,2},{8,10},{16,18},{24,26},{32,34},{40,42},{48,50},{56,58},{64,6... | collective-permute-start | bytes 4128776 | tf_op jit(solution)/shard_map/ppermute | solution.py:384
  26.2 0.7 %collective-permute-start.2 = (f32[384,896]{1,0:T(8,128)S(1)}, f32[384,896]{1,0:T(8,128)S(1)}, u32[]{:S(2)}, u32[]{:S(2)}) collective-permute-start(f32[384,896]{1,0:T(8,128)S(1)} %get-tuple-element.35), channel_id=1, source_target_pairs={{4,6},{12,14},{20,22},{28,30},{36,38},{44,46},{52,54},{60,62},{68,... | collective-permute-start | bytes 4128776 | tf_op jit(solution)/shard_map/ppermute | solution.py:384
  26.9 1.3 %collective-permute-start.4 = (f32[256,384]{1,0:T(8,128)S(1)}, f32[256,384]{1,0:T(8,128)S(1)}, u32[]{:S(2)}, u32[]{:S(2)}) collective-permute-start(f32[256,384]{1,0:T(8,128)S(1)} %get-tuple-element.37), channel_id=1, source_target_pairs={{4,3},{5,2},{12,11},{13,10},{20,19},{21,18},{28,27},{29,26},{36,35... | collective-permute-start | bytes 1179656 | tf_op jit(solution)/shard_map/ppermute | solution.py:388
  28.2 1.3 %collective-permute-start.3 = (f32[384,384]{1,0:T(8,128)S(1)}, f32[384,384]{1,0:T(8,128)S(1)}, u32[]{:S(2)}, u32[]{:S(2)}) collective-permute-start(f32[384,384]{1,0:T(8,128)S(1)} %get-tuple-element.36.u_high), channel_id=1, source_target_pairs={{2,6},{10,14},{18,22},{26,30},{34,38},{42,46},{50,54},{58,62},{66,... | collective-permute-start | bytes 1769480 | tf_op jit(solution)/shard_map/ppermute | solution.py:384
  29.6 1.3 %collective-permute-start.1 = (f32[384,384]{1,0:T(8,128)S(1)}, f32[384,384]{1,0:T(8,128)S(1)}, u32[]{:S(2)}, u32[]{:S(2)}) collective-permute-start(f32[384,384]{1,0:T(8,128)S(1)} %get-tuple-element.34), channel_id=1, source_target_pairs={{2,6},{10,14},{18,22},{26,30},{34,38},{42,46},{50,54},{58,62},{66,... | collective-permute-start | bytes 1769480 | tf_op jit(solution)/shard_map/ppermute | solution.py:384
  30.9 6.3 %collective-permute-done.4.packed_in = f32[256,384]{1,0:T(8,128)S(1)} collective-permute-done((f32[256,384]{1,0:T(8,128)S(1)}, f32[256,384]{1,0:T(8,128)S(1)}, u32[]{:S(2)}, u32[]{:S(2)}) %collective-permute-start.4) | collective-permute-done | bytes 393248 | tf_op jit(solution)/shard_map/ppermute | solution.py:388
  37.2 1.3 %collective-permute-start.6 = (f32[384,128]{1,0:T(8,128)S(1)}, f32[384,128]{1,0:T(8,128)S(1)}, u32[]{:S(2)}, u32[]{:S(2)}) collective-permute-start(f32[384,128]{1,0:T(8,128)S(1)} %get-tuple-element.33.thin), channel_id=1, source_target_pairs={{4,2},{12,10},{20,18},{28,26},{36,34},{44,42},{52,50},{60,58},{68,... | collective-permute-start | bytes 589832 | tf_op jit(solution)/shard_map/ppermute | solution.py:384
  38.5 0.0 collective-permute-done.5.full
  38.5 5.2 %shard_map.55 = (f32[256,384]{1,0:T(8,128)S(1)}, f32[384,384]{1,0:T(8,128)S(1)}, bf16[384,1152]{1,0:T(8,128)(2,1)S(1)}) custom-call(f32[384,384]{1,0:T(8,128)S(1)} %get-tuple-element.32.whole, f32[256,384]{1,0:T(8,128)S(1)} %collective-permute-done.4.packed_in, f32[384,896]{1,0:T(8,128)S(1)} %collective-permute-done.5.full, ...), custom_call_target="tpu_custom_call" | custom-call | flops 2717908992 | bytes 4194304 | tf_op jit(solution)/shard_map/pallas_call | solution.py:441
  43.7 1.3 %collective-permute-start.7 = (f32[256,384]{1,0:T(8,128)S(1)}, f32[256,384]{1,0:T(8,128)S(1)}, u32[]{:S(2)}, u32[]{:S(2)}) collective-permute-start(f32[256,384]{1,0:T(8,128)S(1)} %get-tuple-element.44), channel_id=1, source_target_pairs={{10,7},{11,6},{18,15},{19,14},{26,23},{27,22},{34,31},{35,30},{42,... | collective-permute-start | bytes 1179656 | tf_op jit(solution)/shard_map/ppermute | solution.py:388
  45.1 1.1 %shard_map.56 = (f32[384,128]{1,0:T(8,128)S(1)}, f32[384,128]{1,0:T(8,128)S(1)}) custom-call(bf16[384,1152]{1,0:T(8,128)(2,1)S(1)} %get-tuple-element.39.t_left, f32[384,128]{1,0:T(8,128)S(1)} %get-tuple-element.33.thin, f32[384,128]{1,0:T(8,128)S(1)} %collective-permute-done.6.thin_in, f32[384,896]{1,0:T(8,128)S(1)} %collective-permute-done.5.full, ...), custom_call_target="tpu_custom_call" | custom-call | flops 227624880 | bytes 4194304 | tf_op jit(solution)/shard_map/pallas_call | solution.py:451
  46.2 1.3 %collective-permute-start.8 = (f32[384,128]{1,0:T(8,128)S(1)}, f32[384,128]{1,0:T(8,128)S(1)}, u32[]{:S(2)}, u32[]{:S(2)}) collective-permute-start(f32[384,128]{1,0:T(8,128)S(1)} %get-tuple-element.47), channel_id=1, source_target_pairs={{10,6},{18,14},{26,22},{34,30},{42,38},{50,46},{58,54},{66,62},{74... | collective-permute-start | bytes 589832 | tf_op jit(solution)/shard_map/ppermute | solution.py:384
  47.5 0.0 collective-permute-done.3.u_left
  47.5 0.2 shard_map.54.sums
  47.8 0.9 %shard_map.57 = (f32[384,384]{1,0:T(8,128)S(1)}, f32[384,128]{1,0:T(8,128)S(1)}, bf16[384,1536]{1,0:T(8,128)(2,1)S(1)}, f32[2,384,384]{2,1,0:T(8,128)}, f32[2,384,128]{2,1,0:T(8,128)}) custom-call(f32[384,384]{1,0:T(8,128)S(1)} %get-tuple-element.32.whole, f32[384,128]{1,0:T(8,128)S(1)} %get-tuple-element.33.thin, ...), custom_call_target="tpu_custom_call", output_to_operand_aliasing={{3}: (7, {}), {4}: (8, {})} | custom-call | flops 2150545408 | bytes 4194304 | tf_op jit(solution)/shard_map/pallas_call | solution.py:468
  48.8 1.0 %collective-permute-done.7.packed_in = f32[256,384]{1,0:T(8,128)S(1)} collective-permute-done((f32[256,384]{1,0:T(8,128)S(1)}, f32[256,384]{1,0:T(8,128)S(1)}, u32[]{:S(2)}, u32[]{:S(2)}) %collective-permute-start.7) | collective-permute-done | bytes 393248 | tf_op jit(solution)/shard_map/ppermute | solution.py:388
  49.7 2.1 %collective-permute-done.8.thin_in = f32[384,128]{1,0:T(8,128)S(1)} collective-permute-done((f32[384,128]{1,0:T(8,128)S(1)}, f32[384,128]{1,0:T(8,128)S(1)}, u32[]{:S(2)}, u32[]{:S(2)}) %collective-permute-start.8) | collective-permute-done | bytes 196640 | tf_op jit(solution)/shard_map/ppermute | solution.py:384
  51.8 0.1 shard_map.59
  (4 shorter events, 0.0 us)
Async XLA Ops:
  6.5 11.5 %collective-permute-start = (f32[384,896]{1,0:T(8,128)S(1)}, f32[384,896]{1,0:T(8,128)S(1)}, u32[]{:S(2)}, u32[]{:S(2)}) collective-permute-start(f32[384,896]{1,0:T(8,128)S(1)} %get-tuple-element.27.pay), channel_id=1, source_target_pairs={{0,2},{2,0},{4,6},{6,4},{8,10},{10,8},{12,14},{14,12},{16,18},{18,... | collective-permute-start | bytes 4128776 | tf_op jit(solution)/shard_map/ppermute | solution.py:384
  24.9 13.7 %collective-permute-start.5 = (f32[384,896]{1,0:T(8,128)S(1)}, f32[384,896]{1,0:T(8,128)S(1)}, u32[]{:S(2)}, u32[]{:S(2)}) collective-permute-start(f32[384,896]{1,0:T(8,128)S(1)} %get-tuple-element.35), channel_id=1, source_target_pairs={{0,2},{8,10},{16,18},{24,26},{32,34},{40,42},{48,50},{56,58},{64,6... | collective-permute-start | bytes 4128776 | tf_op jit(solution)/shard_map/ppermute | solution.py:384
  26.2 21.4 %collective-permute-start.2 = (f32[384,896]{1,0:T(8,128)S(1)}, f32[384,896]{1,0:T(8,128)S(1)}, u32[]{:S(2)}, u32[]{:S(2)}) collective-permute-start(f32[384,896]{1,0:T(8,128)S(1)} %get-tuple-element.35), channel_id=1, source_target_pairs={{4,6},{12,14},{20,22},{28,30},{36,38},{44,46},{52,54},{60,62},{68,... | collective-permute-start | bytes 4128776 | tf_op jit(solution)/shard_map/ppermute | solution.py:384
  26.9 10.3 %collective-permute-start.4 = (f32[256,384]{1,0:T(8,128)S(1)}, f32[256,384]{1,0:T(8,128)S(1)}, u32[]{:S(2)}, u32[]{:S(2)}) collective-permute-start(f32[256,384]{1,0:T(8,128)S(1)} %get-tuple-element.37), channel_id=1, source_target_pairs={{4,3},{5,2},{12,11},{13,10},{20,19},{21,18},{28,27},{29,26},{36,35... | collective-permute-start | bytes 1179656 | tf_op jit(solution)/shard_map/ppermute | solution.py:388
  28.2 19.3 %collective-permute-start.3 = (f32[384,384]{1,0:T(8,128)S(1)}, f32[384,384]{1,0:T(8,128)S(1)}, u32[]{:S(2)}, u32[]{:S(2)}) collective-permute-start(f32[384,384]{1,0:T(8,128)S(1)} %get-tuple-element.36.u_high), channel_id=1, source_target_pairs={{2,6},{10,14},{18,22},{26,30},{34,38},{42,46},{50,54},{58,62},{66,... | collective-permute-start | bytes 1769480 | tf_op jit(solution)/shard_map/ppermute | solution.py:384
  29.6 18.2 %collective-permute-start.1 = (f32[384,384]{1,0:T(8,128)S(1)}, f32[384,384]{1,0:T(8,128)S(1)}, u32[]{:S(2)}, u32[]{:S(2)}) collective-permute-start(f32[384,384]{1,0:T(8,128)S(1)} %get-tuple-element.34), channel_id=1, source_target_pairs={{2,6},{10,14},{18,22},{26,30},{34,38},{42,46},{50,54},{58,62},{66,... | collective-permute-start | bytes 1769480 | tf_op jit(solution)/shard_map/ppermute | solution.py:384
  37.2 7.8 %collective-permute-start.6 = (f32[384,128]{1,0:T(8,128)S(1)}, f32[384,128]{1,0:T(8,128)S(1)}, u32[]{:S(2)}, u32[]{:S(2)}) collective-permute-start(f32[384,128]{1,0:T(8,128)S(1)} %get-tuple-element.33.thin), channel_id=1, source_target_pairs={{4,2},{12,10},{20,18},{28,26},{36,34},{44,42},{52,50},{60,58},{68,... | collective-permute-start | bytes 589832 | tf_op jit(solution)/shard_map/ppermute | solution.py:384
  43.7 6.0 %collective-permute-start.7 = (f32[256,384]{1,0:T(8,128)S(1)}, f32[256,384]{1,0:T(8,128)S(1)}, u32[]{:S(2)}, u32[]{:S(2)}) collective-permute-start(f32[256,384]{1,0:T(8,128)S(1)} %get-tuple-element.44), channel_id=1, source_target_pairs={{10,7},{11,6},{18,15},{19,14},{26,23},{27,22},{34,31},{35,30},{42,... | collective-permute-start | bytes 1179656 | tf_op jit(solution)/shard_map/ppermute | solution.py:388
  46.2 5.6 %collective-permute-start.8 = (f32[384,128]{1,0:T(8,128)S(1)}, f32[384,128]{1,0:T(8,128)S(1)}, u32[]{:S(2)}, u32[]{:S(2)}) collective-permute-start(f32[384,128]{1,0:T(8,128)S(1)} %get-tuple-element.47), channel_id=1, source_target_pairs={{10,6},{18,14},{26,22},{34,30},{42,38},{50,46},{58,54},{66,62},{74... | collective-permute-start | bytes 589832 | tf_op jit(solution)/shard_map/ppermute | solution.py:384

commit v5 on v4

--- a/solution.py
+++ b/solution.py
@@ -212,29 +212,38 @@
         pack(packed, whole)
 
 
+def updated(of_d, of_x, left, right, u_b, r_b):
+    put_left(left, of_d[:, N : 2 * N])
+    put_right(right, of_x[:, N:W])
+    u_b[...] = -dot(left[...], right[:, 0:N])
+    r_b[...] = of_d[:, 2 * N : W] - dot(left[...], right[:, N : N + C])
+
+
+def keep_last(keep, x_b, u_b, r_b, whole, thin, both, left, right):
+    put_both(both, u_b[...].T)
+    put_right(right, x_b[...], 0)
+    put_left(left, dot(as_left(both), right[:, 0:N]))
+    put_right(right, r_b[...], N)
+    whole[...] = keep[:, 0:N] - dot_t(left[...], as_right_t(both))
+    thin[...] = keep[:, 2 * N : W] - dot(left[...], right[:, N : N + C])
+
+
 def spread_kernel(
     t_left, pay, recv, keep, s_in, x_b, inv_in, rhs_in,
     full, packed, whole, thin, inv_out, rhs_out, both, left, right, u_b, r_b, sems
 ):
     del inv_in, rhs_in
-    at_low = (lax.axis_index("layer") % 2) == 0
-    stores = [
-        pltpu.make_async_copy(x_b, inv_out.at[1], sems.at[0]),
-        pltpu.make_async_copy(r_b, rhs_out.at[1], sems.at[1]),
-    ]
-
-    def step(of_d, of_x):
-        put_left(left, of_d[:, N : 2 * N])
-        put_right(right, of_x[:, N:W])
-        u_b[...] = -dot(left[...], right[:, 0:N])
-        r_b[...] = of_d[:, 2 * N : W] - dot(left[...], right[:, N : N + C])
-
-    by_role(step, pay, recv)
-
-    @pl.when(at_low)
-    def _():
-        for store in stores:
-            store.start()
+    place = lax.axis_index("layer") % 4
+
+    @pl.when(place % 2 == 0)
+    def _():
+        stores = [
+            pltpu.make_async_copy(x_b, inv_out.at[1], sems.at[0]),
+            pltpu.make_async_copy(r_b, rhs_out.at[1], sems.at[1]),
+        ]
+        stores[0].start()
+        updated(pay, recv, left, right, u_b, r_b)
+        stores[1].start()
         put_right(right, u_b[...], 0)
         put_right(right, r_b[...], N)
         full[:, N : 2 * N] = dot(t_left[...], right[:, 0:N])
@@ -244,14 +253,10 @@
         for store in stores:
             store.wait()
 
-    @pl.when(jnp.logical_not(at_low))
-    def _():
-        put_both(both, u_b[...].T)
-        put_right(right, x_b[...], 0)
-        put_left(left, dot(as_left(both), right[:, 0:N]))
-        put_right(right, r_b[...], N)
-        whole[...] = keep[:, 0:N] - dot_t(left[...], as_right_t(both))
-        thin[...] = keep[:, 2 * N : W] - dot(left[...], right[:, N : N + C])
+    @pl.when(place == 1)
+    def _():
+        updated(recv, pay, left, right, u_b, r_b)
+        keep_last(keep, x_b, u_b, r_b, whole, thin, both, left, right)
         pack(packed, whole)
         pack_rhs(packed, thin)
 
@@ -281,9 +286,11 @@
         thin_out[...] = full[:, 2 * N : W] + dot(t_left[...], right[...])
 
 
-def left_kernel(full, u_left, sums, both, left, right):
+def left_kernel(full, u_left, pay, recv, keep, x_b, sums, whole, thin, both, left, right, u_b, r_b):
     @pl.when(lax.axis_index("layer") % 4 == 3)
     def _():
+        updated(recv, pay, left, right, u_b, r_b)
+        keep_last(keep, x_b, u_b, r_b, whole, thin, both, left, right)
         put_both(both, u_left[...])
         put_right(right, full[...])
         sums[...] = dot(as_left(both), right[...])
@@ -382,10 +389,6 @@
 
     def send(block, route):
         return lax.ppermute(block, "layer", [(i % size, j % size) for i, j in route])
-
-    def send_crossed(block, route):
-        pairs = [(2 * (i % size) + c, 2 * (j % size) + 1 - c) for i, j in route for c in (0, 1)]
-        return lax.ppermute(block, ("layer", "rhs"), pairs)
 
     wide = pltpu.VMEM((3 * N, W), BF16)
     mid = pltpu.VMEM((3 * N, N + C), BF16)
@@ -425,7 +428,7 @@
         [double, tall],
         2,
     )(keep, x_b)
-    urgent_in = send_crossed(packed, [(4 * g + 2, 4 * g + 1) for g in groups])
+    urgent_in = send(packed, [(4 * g + 2, 4 * g + 1) for g in groups])
     full, packed, whole, thin, inv_out, rhs_out = call(
         spread_kernel,
         (like(N, W), like(N, N), like(N, N), like(N, C), *outputs),
@@ -447,7 +450,8 @@
         8,
     )(whole, urgent_in, full_in, u_high)
     down = [(4 * g + 5, 4 * g + 3) for g in groups]
-    last_in = send_crossed(packed, down)
+    crossed = [(2 * (i % size) + c, 2 * (j % size) + 1 - c) for i, j in down for c in (0, 1)]
+    last_in = lax.ppermute(packed, ("layer", "rhs"), crossed)
     down_thin, r_3 = call(
         rest_kernel,
         (like(N, C), like(N, C)),
@@ -457,14 +461,15 @@
         0.67,
     )(t_left, thin, thin_in, full_in, u_high)
     thin_in = send(down_thin, down)
-    sums = call(
+    full_b = send(full, [(4 * g + 2, 4 * g + 3) for g in groups])
+    sums, whole, thin = call(
         left_kernel,
-        like(N, W),
-        vmem(),
-        [vmem()] * 2,
-        [double, flat, wide],
-        3.33,
-    )(send(full, [(4 * g + 2, 4 * g + 3) for g in groups]), u_left)
+        (like(N, W), like(N, N), like(N, C)),
+        (vmem(),) * 3,
+        [vmem()] * 6,
+        [double, flat, wide, tile, strip],
+        7,
+    )(full_b, u_left, pay, recv, keep, x_b)
     whole, thin, u_both, inv_out, rhs_out = call(
         fifth_kernel,
         (like(N, N), like(N, C), jax.ShapeDtypeStruct((N, 4 * N), BF16), *outputs),

time: 52.7 us -> 52.6 us (level)
  the two profiles are of different devices: /device:TPU:1 before, /device:TPU:3 now
where the time goes in v5:
time: 52.6 us; the launch traced here: 52.3 us
  Pallas kernels  23.8 us (45%)
  waiting for transfers between devices  16.3 us (31%)
  starting transfers between devices  11.2 us (21%)
  between operations  0.99 us (2%)
    ppermute x8, waiting for transfers between devices, send(): lax.ppermute(block, 'layer', [(i % size, j % size) for i, j in route])  16.3 us
    ppermute x8, starting transfers between devices, send(): lax.ppermute(block, 'layer', [(i % size, j % size) for i, j in route])  9.9 us
    pallas_call x1, Pallas kernels, reduce_chain(): call(first_kernel, (like(N, W), like(N, W), like(N, N), *outputs), (vmem(...  5.87 us
    pallas_call x1, Pallas kernels, reduce_chain(): call(fifth_kernel, (like(N, N), like(N, C), jax.ShapeDtypeStruct((N, 4 *...  4.57 us
    pallas_call x1, Pallas kernels, reduce_chain(): call(left_kernel, (like(N, W), like(N, N), like(N, C)), (vmem(),) * 3, [v...  4 us
    pallas_call x1, Pallas kernels, reduce_chain(): call(sixth_kernel, like(N, N), vmem(), [vmem()] * 3, [flat, tall, tile, *...  4 us
    pallas_call x1, Pallas kernels, reduce_chain(): call(second_kernel, like(N, N), vmem(), [vmem()] * 2, [double, flat, tall...  3.86 us
    ppermute x1, starting transfers between devices, reduce_chain(): last_in = lax.ppermute(packed, ('layer', 'rhs'), crossed)  1.29 us
  transfers between devices with their start and end apart: 9, of which 3 were waited for; matrix products, arithmetic and copies ran while one was open for 0% of the time, Pallas kernels for 24%

profile of v5, /device:TPU:3, one launch (start us, length us, event | category | flops | bytes accessed | tf_op | source)
XLA Modules:
  0.0 52.3 jit_solution(16200521888828801871)
XLA Ops:
  0.6 5.9 %shard_map.50 = (f32[384,896]{1,0:T(8,128)S(1)}, f32[384,896]{1,0:T(8,128)S(1)}, f32[384,384]{1,0:T(8,128)S(1)}, f32[2,384,384]{2,1,0:T(8,128)}, f32[2,384,128]{2,1,0:T(8,128)}) custom-call(f32[2,384,384]{2,1,0:T(8,128)} %diag.1, f32[2,384,384]{2,1,0:T(8,128)} %coup.1, f32[2,384,128]{2,1,0:T(8,128)} %rhs.1), custom_call_target="tpu_custom_call" | custom-call | flops 2266056704 | bytes 4194304 | tf_op jit(solution)/shard_map/pallas_call | solution.py:405
  6.5 2.6 %collective-permute-start = (f32[384,896]{1,0:T(8,128)S(1)}, f32[384,896]{1,0:T(8,128)S(1)}, u32[]{:S(2)}, u32[]{:S(2)}) collective-permute-start(f32[384,896]{1,0:T(8,128)S(1)} %get-tuple-element.30.pay), channel_id=1, source_target_pairs={{0,2},{2,0},{4,6},{6,4},{8,10},{10,8},{12,14},{14,12},{16,18},{18,... | collective-permute-start | bytes 4128776 | tf_op jit(solution)/shard_map/ppermute | solution.py:391
  9.1 2.7 %collective-permute-done.recv = f32[384,896]{1,0:T(8,128)S(1)} collective-permute-done((f32[384,896]{1,0:T(8,128)S(1)}, f32[384,896]{1,0:T(8,128)S(1)}, u32[]{:S(2)}, u32[]{:S(2)}) %collective-permute-start) | collective-permute-done | bytes 1376288 | tf_op jit(solution)/shard_map/ppermute | solution.py:391
  11.9 3.9 %shard_map.51.x_b = f32[384,384]{1,0:T(8,128)S(1)} custom-call(f32[384,896]{1,0:T(8,128)S(1)} %get-tuple-element.30.pay, f32[384,896]{1,0:T(8,128)S(1)} %collective-permute-done.recv), custom_call_target="tpu_custom_call" | custom-call | flops 2038431744 | bytes 4194304 | tf_op jit(solution)/shard_map/pallas_call | solution.py:415
  15.7 0.2 shard_map.52
  16.0 0.1 shard_map.53
  16.1 0.7 %collective-permute-start.5 = (f32[384,896]{1,0:T(8,128)S(1)}, f32[384,896]{1,0:T(8,128)S(1)}, u32[]{:S(2)}, u32[]{:S(2)}) collective-permute-start(f32[384,896]{1,0:T(8,128)S(1)} %get-tuple-element.35), channel_id=1, source_target_pairs={{0,2},{8,10},{16,18},{24,26},{32,34},{40,42},{48,50},{56,58},{64,6... | collective-permute-start | bytes 4128776 | tf_op jit(solution)/shard_map/ppermute | solution.py:391
  16.8 1.3 %collective-permute-start.1 = (f32[384,896]{1,0:T(8,128)S(1)}, f32[384,896]{1,0:T(8,128)S(1)}, u32[]{:S(2)}, u32[]{:S(2)}) collective-permute-start(f32[384,896]{1,0:T(8,128)S(1)} %get-tuple-element.35), channel_id=1, source_target_pairs={{4,6},{12,14},{20,22},{28,30},{36,38},{44,46},{52,54},{60,62},{68,... | collective-permute-start | bytes 4128776 | tf_op jit(solution)/shard_map/ppermute | solution.py:391
  18.1 0.7 %collective-permute-start.4 = (f32[256,384]{1,0:T(8,128)S(1)}, f32[256,384]{1,0:T(8,128)S(1)}, u32[]{:S(2)}, u32[]{:S(2)}) collective-permute-start(f32[256,384]{1,0:T(8,128)S(1)} %get-tuple-element.42), channel_id=1, source_target_pairs={{4,2},{12,10},{20,18},{28,26},{36,34},{44,42},{52,50},{60,58},{68,... | collective-permute-start | bytes 1179656 | tf_op jit(solution)/shard_map/ppermute | solution.py:391
  18.8 1.3 %collective-permute-start.2 = (f32[384,384]{1,0:T(8,128)S(1)}, f32[384,384]{1,0:T(8,128)S(1)}, u32[]{:S(2)}, u32[]{:S(2)}) collective-permute-start(f32[384,384]{1,0:T(8,128)S(1)} %get-tuple-element.36.u_high), channel_id=1, source_target_pairs={{2,6},{10,14},{18,22},{26,30},{34,38},{42,46},{50,54},{58,62},{66,... | collective-permute-start | bytes 1769480 | tf_op jit(solution)/shard_map/ppermute | solution.py:391
  20.1 1.3 %collective-permute-start.3 = (f32[384,384]{1,0:T(8,128)S(1)}, f32[384,384]{1,0:T(8,128)S(1)}, u32[]{:S(2)}, u32[]{:S(2)}) collective-permute-start(f32[384,384]{1,0:T(8,128)S(1)} %get-tuple-element.39), channel_id=1, source_target_pairs={{2,6},{10,14},{18,22},{26,30},{34,38},{42,46},{50,54},{58,62},{66,... | collective-permute-start | bytes 1769480 | tf_op jit(solution)/shard_map/ppermute | solution.py:391
  21.4 0.0 collective-permute-done.4.packed_in
  21.4 0.7 %collective-permute-start.6 = (f32[384,128]{1,0:T(8,128)S(1)}, f32[384,128]{1,0:T(8,128)S(1)}, u32[]{:S(2)}, u32[]{:S(2)}) collective-permute-start(f32[384,128]{1,0:T(8,128)S(1)} %get-tuple-element.45.thin), channel_id=1, source_target_pairs={{4,2},{12,10},{20,18},{28,26},{36,34},{44,42},{52,50},{60,58},{68,... | collective-permute-start | bytes 589832 | tf_op jit(solution)/shard_map/ppermute | solution.py:391
  22.1 0.0 collective-permute-done.5.full
  22.1 1.3 %collective-permute-start.7 = (f32[256,384]{1,0:T(8,128)S(1)}, f32[256,384]{1,0:T(8,128)S(1)}, u32[]{:S(2)}, u32[]{:S(2)}) collective-permute-start(f32[256,384]{1,0:T(8,128)S(1)} %get-tuple-element.50), channel_id=1, source_target_pairs={{10,7},{11,6},{18,15},{19,14},{26,23},{27,22},{34,31},{35,30},{42,... | collective-permute-start | bytes 1179656 | tf_op jit(solution)/shard_map/ppermute | solution.py:454
  23.4 0.0 collective-permute-done.6.thin_in
  23.5 1.3 %collective-permute-start.8 = (f32[384,128]{1,0:T(8,128)S(1)}, f32[384,128]{1,0:T(8,128)S(1)}, u32[]{:S(2)}, u32[]{:S(2)}) collective-permute-start(f32[384,128]{1,0:T(8,128)S(1)} %get-tuple-element.53), channel_id=1, source_target_pairs={{10,6},{18,14},{26,22},{34,30},{42,38},{50,46},{58,54},{66,62},{74... | collective-permute-start | bytes 589832 | tf_op jit(solution)/shard_map/ppermute | solution.py:391
  24.8 11.3 %collective-permute-done.2.u_left = f32[384,384]{1,0:T(8,128)S(1)} collective-permute-done((f32[384,384]{1,0:T(8,128)S(1)}, f32[384,384]{1,0:T(8,128)S(1)}, u32[]{:S(2)}, u32[]{:S(2)}) %collective-permute-start.2) | collective-permute-done | bytes 589856 | tf_op jit(solution)/shard_map/ppermute | solution.py:391
  36.0 0.0 collective-permute-done.1.full
  36.0 4.0 %shard_map.54 = (f32[384,896]{1,0:T(8,128)S(1)}, f32[384,384]{1,0:T(8,128)S(1)}, f32[384,128]{1,0:T(8,128)S(1)}) custom-call(f32[384,896]{1,0:T(8,128)S(1)} %collective-permute-done.1.full, f32[384,384]{1,0:T(8,128)S(1)} %collective-permute-done.2.u_left, f32[384,896]{1,0:T(8,128)S(1)} %get-tuple-element.30.pay, f32[384,896]{1,0:T(8,128)S(1)} %collective-permute-done.recv, ...), custom_call_target="tpu_custom_call" | custom-call | flops 2378170368 | bytes 4194304 | tf_op jit(solution)/shard_map/pallas_call | solution.py:465
  40.0 2.3 %collective-permute-done.3.packed_in = f32[384,384]{1,0:T(8,128)S(1)} collective-permute-done((f32[384,384]{1,0:T(8,128)S(1)}, f32[384,384]{1,0:T(8,128)S(1)}, u32[]{:S(2)}, u32[]{:S(2)}) %collective-permute-start.3) | collective-permute-done | bytes 589856 | tf_op jit(solution)/shard_map/ppermute | solution.py:391
  42.4 4.6 %shard_map.57 = (f32[384,384]{1,0:T(8,128)S(1)}, f32[384,128]{1,0:T(8,128)S(1)}, bf16[384,1536]{1,0:T(8,128)(2,1)S(1)}, f32[2,384,384]{2,1,0:T(8,128)}, f32[2,384,128]{2,1,0:T(8,128)}) custom-call(f32[384,384]{1,0:T(8,128)S(1)} %get-tuple-element.37.whole, f32[384,128]{1,0:T(8,128)S(1)} %get-tuple-element.38.thin, ...), custom_call_target="tpu_custom_call", output_to_operand_aliasing={{3}: (7, {}), {4}: (8, {})} | custom-call | flops 2150545408 | bytes 4194304 | tf_op jit(solution)/shard_map/pallas_call | solution.py:473
  46.9 4.0 %shard_map.58.x_in = f32[384,384]{1,0:T(8,128)S(1)} custom-call(f32[384,384]{1,0:T(8,128)S(1)} %get-tuple-element.49.whole, f32[256,384]{1,0:T(8,128)S(1)} %collective-permute-done.7.packed_in, bf16[384,1536]{1,0:T(8,128)(2,1)S(1)} %get-tuple-element.51.u_both), custom_call_target="tpu_custom_call" | custom-call | flops 2038431744 | bytes 4194304 | tf_op jit(solution)/shard_map/pallas_call | solution.py:482
  51.0 1.2 %shard_map.59 = (f32[2,384,384]{2,1,0:T(8,128)}, f32[2,384,128]{2,1,0:T(8,128)}) custom-call(f32[384,384]{1,0:T(8,128)S(1)} %shard_map.58.x_in, f32[384,128]{1,0:T(8,128)S(1)} %get-tuple-element.52.thin, f32[384,128]{1,0:T(8,128)S(1)} %collective-permute-done.8.thin_in, ...), custom_call_target="tpu_custom_call", output_to_operand_aliasing={{0}: (4, {}), {1}: (5, {})} | custom-call | flops 112113744 | bytes 4194304 | tf_op jit(solution)/shard_map/pallas_call | solution.py:490
  (4 shorter events, 0.0 us)
Async XLA Ops:
  6.5 5.4 %collective-permute-start = (f32[384,896]{1,0:T(8,128)S(1)}, f32[384,896]{1,0:T(8,128)S(1)}, u32[]{:S(2)}, u32[]{:S(2)}) collective-permute-start(f32[384,896]{1,0:T(8,128)S(1)} %get-tuple-element.30.pay), channel_id=1, source_target_pairs={{0,2},{2,0},{4,6},{6,4},{8,10},{10,8},{12,14},{14,12},{16,18},{18,... | collective-permute-start | bytes 4128776 | tf_op jit(solution)/shard_map/ppermute | solution.py:391
  16.1 6.0 %collective-permute-start.5 = (f32[384,896]{1,0:T(8,128)S(1)}, f32[384,896]{1,0:T(8,128)S(1)}, u32[]{:S(2)}, u32[]{:S(2)}) collective-permute-start(f32[384,896]{1,0:T(8,128)S(1)} %get-tuple-element.35), channel_id=1, source_target_pairs={{0,2},{8,10},{16,18},{24,26},{32,34},{40,42},{48,50},{56,58},{64,6... | collective-permute-start | bytes 4128776 | tf_op jit(solution)/shard_map/ppermute | solution.py:391
  16.8 19.2 %collective-permute-start.1 = (f32[384,896]{1,0:T(8,128)S(1)}, f32[384,896]{1,0:T(8,128)S(1)}, u32[]{:S(2)}, u32[]{:S(2)}) collective-permute-start(f32[384,896]{1,0:T(8,128)S(1)} %get-tuple-element.35), channel_id=1, source_target_pairs={{4,6},{12,14},{20,22},{28,30},{36,38},{44,46},{52,54},{60,62},{68,... | collective-permute-start | bytes 4128776 | tf_op jit(solution)/shard_map/ppermute | solution.py:391
  18.1 3.3 %collective-permute-start.4 = (f32[256,384]{1,0:T(8,128)S(1)}, f32[256,384]{1,0:T(8,128)S(1)}, u32[]{:S(2)}, u32[]{:S(2)}) collective-permute-start(f32[256,384]{1,0:T(8,128)S(1)} %get-tuple-element.42), channel_id=1, source_target_pairs={{4,2},{12,10},{20,18},{28,26},{36,34},{44,42},{52,50},{60,58},{68,... | collective-permute-start | bytes 1179656 | tf_op jit(solution)/shard_map/ppermute | solution.py:391
  18.8 17.2 %collective-permute-start.2 = (f32[384,384]{1,0:T(8,128)S(1)}, f32[384,384]{1,0:T(8,128)S(1)}, u32[]{:S(2)}, u32[]{:S(2)}) collective-permute-start(f32[384,384]{1,0:T(8,128)S(1)} %get-tuple-element.36.u_high), channel_id=1, source_target_pairs={{2,6},{10,14},{18,22},{26,30},{34,38},{42,46},{50,54},{58,62},{66,... | collective-permute-start | bytes 1769480 | tf_op jit(solution)/shard_map/ppermute | solution.py:391
  20.1 22.2 %collective-permute-start.3 = (f32[384,384]{1,0:T(8,128)S(1)}, f32[384,384]{1,0:T(8,128)S(1)}, u32[]{:S(2)}, u32[]{:S(2)}) collective-permute-start(f32[384,384]{1,0:T(8,128)S(1)} %get-tuple-element.39), channel_id=1, source_target_pairs={{2,6},{10,14},{18,22},{26,30},{34,38},{42,46},{50,54},{58,62},{66,... | collective-permute-start | bytes 1769480 | tf_op jit(solution)/shard_map/ppermute | solution.py:391
  21.4 2.0 %collective-permute-start.6 = (f32[384,128]{1,0:T(8,128)S(1)}, f32[384,128]{1,0:T(8,128)S(1)}, u32[]{:S(2)}, u32[]{:S(2)}) collective-permute-start(f32[384,128]{1,0:T(8,128)S(1)} %get-tuple-element.45.thin), channel_id=1, source_target_pairs={{4,2},{12,10},{20,18},{28,26},{36,34},{44,42},{52,50},{60,58},{68,... | collective-permute-start | bytes 589832 | tf_op jit(solution)/shard_map/ppermute | solution.py:391
  22.1 24.8 %collective-permute-start.7 = (f32[256,384]{1,0:T(8,128)S(1)}, f32[256,384]{1,0:T(8,128)S(1)}, u32[]{:S(2)}, u32[]{:S(2)}) collective-permute-start(f32[256,384]{1,0:T(8,128)S(1)} %get-tuple-element.50), channel_id=1, source_target_pairs={{10,7},{11,6},{18,15},{19,14},{26,23},{27,22},{34,31},{35,30},{42,... | collective-permute-start | bytes 1179656 | tf_op jit(solution)/shard_map/ppermute | solution.py:454
  23.5 27.5 %collective-permute-start.8 = (f32[384,128]{1,0:T(8,128)S(1)}, f32[384,128]{1,0:T(8,128)S(1)}, u32[]{:S(2)}, u32[]{:S(2)}) collective-permute-start(f32[384,128]{1,0:T(8,128)S(1)} %get-tuple-element.53), channel_id=1, source_target_pairs={{10,6},{18,14},{26,22},{34,30},{42,38},{50,46},{58,54},{66,62},{74... | collective-permute-start | bytes 589832 | tf_op jit(solution)/shard_map/ppermute | solution.py:391

commit v6 on v5

--- a/solution.py
+++ b/solution.py
@@ -119,6 +119,18 @@
     out[2 * C : N, C : 2 * C] = packed[C : 2 * C, C : 2 * C].T
 
 
+def put_right_packed(ref, packed):
+    blocks = {(0, j): packed[0:C, j * C : (j + 1) * C] for j in range(3)}
+    blocks |= {(1, j): packed[C : 2 * C, (j - 1) * C : j * C] for j in (1, 2)}
+    blocks[2, 2] = packed[C : 2 * C, 2 * C : N]
+    for (i, j), x in blocks.items():
+        for row, col, part in ((i, j, x), (j, i, x.T))[: 1 + (i != j)]:
+            high, low = halves(part)
+            at = slice(col * C, (col + 1) * C)
+            for third, half in enumerate((high, low, high)):
+                ref[third * N + row * C : third * N + (row + 1) * C, at] = half
+
+
 def pack_rhs(out, x):
     for i in range(3):
         out[2 * C : N, i * C : (i + 1) * C] = x[i * C : (i + 1) * C, :]
@@ -191,7 +203,7 @@
         step(recv, pay)
 
 
-def second_kernel(pay, recv, x_b, both, left, right, d_s, *inv_scratch):
+def second_kernel(pay, recv, keep, x_b, packed, whole, t_left, both, left, right, d_s, *inv_scratch):
     def step(of_d, of_x):
         put_both(both, of_d[:, N : 2 * N])
         put_right(right, of_x[:, 0:N])
@@ -201,8 +213,6 @@
     by_role(step, pay, recv)
     invert(d_s, x_b, *inv_scratch)
 
-
-def third_kernel(keep, x_b, packed, whole, t_left, both, right):
     @pl.when((lax.axis_index("layer") % 2) == 0)
     def _():
         put_both(both, keep[:, N : 2 * N])
@@ -265,8 +275,7 @@
     @pl.when(lax.axis_index("layer") % 4 == 1)
     def _():
         put_both(both, u_high[...])
-        unpack(d_s, packed_in)
-        put_right(right, d_s[...])
+        put_right_packed(right, packed_in)
         put_left(left, dot(as_left(both), right[...]))
         d_s[...] = whole[...] - dot_t(left[...], as_right_t(both))
         invert(d_s, x_out, *inv_scratch, beside=lambda: put_both(both, full[:, N : 2 * N]))
@@ -334,8 +343,7 @@
 def sixth_kernel(whole, packed_in, u_both, x_out, left, right, d_s, *inv_scratch):
     @pl.when(lax.axis_index("layer") % 4 == 3)
     def _():
-        unpack(d_s, packed_in)
-        put_right(right, d_s[...])
+        put_right_packed(right, packed_in)
         put_left(left, dot(as_left(u_both), right[...]))
         d_s[...] = whole[...] - dot_t(left[...], as_right_t(u_both))
         invert(d_s, x_out, *inv_scratch)
@@ -412,22 +420,14 @@
     )(*[pltpu.with_memory_space_constraint(x, pltpu.HBM) for x in (diag_block, coupling, right_side)])
     recv = send(pay, [(i, i ^ 1) for i in range(size)])
     u_left = send(u_high, [(4 * g + 1, 4 * g + 3) for g in groups])
-    x_b = call(
+    x_b, packed, whole, t_left = call(
         second_kernel,
-        like(N, N),
-        vmem(),
-        [vmem()] * 2,
+        (like(N, N), triangle, like(N, N), half_form),
+        (vmem(),) * 4,
+        [vmem()] * 3,
         [double, flat, tall, tile, *INVERT_SCRATCH],
-        6,
-    )(pay, recv)
-    packed, whole, t_left = call(
-        third_kernel,
-        (triangle, like(N, N), half_form),
-        (vmem(),) * 3,
-        [vmem()] * 2,
-        [double, tall],
-        2,
-    )(keep, x_b)
+        8,
+    )(pay, recv, keep)
     urgent_in = send(packed, [(4 * g + 2, 4 * g + 1) for g in groups])
     full, packed, whole, thin, inv_out, rhs_out = call(
         spread_kernel,

time: 52.6 us -> 52.6 us (level)
    pallas_call x2 -> x1, Pallas kernels: 4.07 us -> 4.05 us  [reduce_chain(): call(second_kernel, (like(N, N), triangle, like(N, N), half_form), (vmem(...]
where the time goes in v6:
time: 52.6 us; the launch traced here: 52.3 us
  Pallas kernels  23.8 us (45%)
  waiting for transfers between devices  16.3 us (31%)
  starting transfers between devices  11.2 us (21%)
  between operations  0.99 us (2%)
    ppermute x8, waiting for transfers between devices, send(): lax.ppermute(block, 'layer', [(i % size, j % size) for i, j in route])  16.3 us
    ppermute x8, starting transfers between devices, send(): lax.ppermute(block, 'layer', [(i % size, j % size) for i, j in route])  9.9 us
    pallas_call x1, Pallas kernels, reduce_chain(): call(first_kernel, (like(N, W), like(N, W), like(N, N), *outputs), (vmem(...  5.87 us
    pallas_call x1, Pallas kernels, reduce_chain(): call(fifth_kernel, (like(N, N), like(N, C), jax.ShapeDtypeStruct((N, 4 *...  4.57 us
    pallas_call x1, Pallas kernels, reduce_chain(): call(second_kernel, (like(N, N), triangle, like(N, N), half_form), (vmem(...  4.05 us
    pallas_call x1, Pallas kernels, reduce_chain(): call(sixth_kernel, like(N, N), vmem(), [vmem()] * 3, [flat, tall, tile, *...  4.02 us
    pallas_call x1, Pallas kernels, reduce_chain(): call(left_kernel, (like(N, W), like(N, N), like(N, C)), (vmem(),) * 3, [v...  4.01 us
    ppermute x1, starting transfers between devices, reduce_chain(): last_in = lax.ppermute(packed, ('layer', 'rhs'), crossed)  1.29 us
  transfers between devices with their start and end apart: 9, of which 3 were waited for; matrix products, arithmetic and copies ran while one was open for 0% of the time, Pallas kernels for 24%

profile of v6, /device:TPU:3, one launch (start us, length us, event | category | flops | bytes accessed | tf_op | source)
XLA Modules:
  0.0 52.3 jit_solution(4040577877495473531)
XLA Ops:
  0.6 5.9 %shard_map.50 = (f32[384,896]{1,0:T(8,128)S(1)}, f32[384,896]{1,0:T(8,128)S(1)}, f32[384,384]{1,0:T(8,128)S(1)}, f32[2,384,384]{2,1,0:T(8,128)}, f32[2,384,128]{2,1,0:T(8,128)}) custom-call(f32[2,384,384]{2,1,0:T(8,128)} %diag.1, f32[2,384,384]{2,1,0:T(8,128)} %coup.1, f32[2,384,128]{2,1,0:T(8,128)} %rhs.1), custom_call_target="tpu_custom_call" | custom-call | flops 2266056704 | bytes 4194304 | tf_op jit(solution)/shard_map/pallas_call | solution.py:413
  6.5 2.6 %collective-permute-start = (f32[384,896]{1,0:T(8,128)S(1)}, f32[384,896]{1,0:T(8,128)S(1)}, u32[]{:S(2)}, u32[]{:S(2)}) collective-permute-start(f32[384,896]{1,0:T(8,128)S(1)} %get-tuple-element.30.pay), channel_id=1, source_target_pairs={{0,2},{2,0},{4,6},{6,4},{8,10},{10,8},{12,14},{14,12},{16,18},{18,... | collective-permute-start | bytes 4128776 | tf_op jit(solution)/shard_map/ppermute | solution.py:399
  9.1 2.7 %collective-permute-done.recv = f32[384,896]{1,0:T(8,128)S(1)} collective-permute-done((f32[384,896]{1,0:T(8,128)S(1)}, f32[384,896]{1,0:T(8,128)S(1)}, u32[]{:S(2)}, u32[]{:S(2)}) %collective-permute-start) | collective-permute-done | bytes 1376288 | tf_op jit(solution)/shard_map/ppermute | solution.py:399
  11.9 4.0 %shard_map.51 = (f32[384,384]{1,0:T(8,128)S(1)}, f32[256,384]{1,0:T(8,128)S(1)}, f32[384,384]{1,0:T(8,128)S(1)}, bf16[384,1152]{1,0:T(8,128)(2,1)S(1)}) custom-call(f32[384,896]{1,0:T(8,128)S(1)} %get-tuple-element.30.pay, f32[384,896]{1,0:T(8,128)S(1)} %collective-permute-done.recv, f32[384,896]{1,0:T(8,128)S(1)} %get-tuple-element.31.keep), custom_call_target="tpu_custom_call" | custom-call | flops 2717908992 | bytes 4194304 | tf_op jit(solution)/shard_map/pallas_call | solution.py:423
  15.9 0.1 shard_map.52
  16.0 0.7 %collective-permute-start.5 = (f32[384,896]{1,0:T(8,128)S(1)}, f32[384,896]{1,0:T(8,128)S(1)}, u32[]{:S(2)}, u32[]{:S(2)}) collective-permute-start(f32[384,896]{1,0:T(8,128)S(1)} %get-tuple-element.37), channel_id=1, source_target_pairs={{0,2},{8,10},{16,18},{24,26},{32,34},{40,42},{48,50},{56,58},{64,6... | collective-permute-start | bytes 4128776 | tf_op jit(solution)/shard_map/ppermute | solution.py:399
  16.8 1.3 %collective-permute-start.1 = (f32[384,896]{1,0:T(8,128)S(1)}, f32[384,896]{1,0:T(8,128)S(1)}, u32[]{:S(2)}, u32[]{:S(2)}) collective-permute-start(f32[384,896]{1,0:T(8,128)S(1)} %get-tuple-element.37), channel_id=1, source_target_pairs={{4,6},{12,14},{20,22},{28,30},{36,38},{44,46},{52,54},{60,62},{68,... | collective-permute-start | bytes 4128776 | tf_op jit(solution)/shard_map/ppermute | solution.py:399
  18.1 0.7 %collective-permute-start.4 = (f32[256,384]{1,0:T(8,128)S(1)}, f32[256,384]{1,0:T(8,128)S(1)}, u32[]{:S(2)}, u32[]{:S(2)}) collective-permute-start(f32[256,384]{1,0:T(8,128)S(1)} %get-tuple-element.44), channel_id=1, source_target_pairs={{4,2},{12,10},{20,18},{28,26},{36,34},{44,42},{52,50},{60,58},{68,... | collective-permute-start | bytes 1179656 | tf_op jit(solution)/shard_map/ppermute | solution.py:399
  18.8 1.3 %collective-permute-start.2 = (f32[384,384]{1,0:T(8,128)S(1)}, f32[384,384]{1,0:T(8,128)S(1)}, u32[]{:S(2)}, u32[]{:S(2)}) collective-permute-start(f32[384,384]{1,0:T(8,128)S(1)} %get-tuple-element.38.u_high), channel_id=1, source_target_pairs={{2,6},{10,14},{18,22},{26,30},{34,38},{42,46},{50,54},{58,62},{66,... | collective-permute-start | bytes 1769480 | tf_op jit(solution)/shard_map/ppermute | solution.py:399
  20.1 1.3 %collective-permute-start.3 = (f32[384,384]{1,0:T(8,128)S(1)}, f32[384,384]{1,0:T(8,128)S(1)}, u32[]{:S(2)}, u32[]{:S(2)}) collective-permute-start(f32[384,384]{1,0:T(8,128)S(1)} %get-tuple-element.41), channel_id=1, source_target_pairs={{2,6},{10,14},{18,22},{26,30},{34,38},{42,46},{50,54},{58,62},{66,... | collective-permute-start | bytes 1769480 | tf_op jit(solution)/shard_map/ppermute | solution.py:399
  21.4 0.0 collective-permute-done.4.packed_in
  21.4 0.7 %collective-permute-start.6 = (f32[384,128]{1,0:T(8,128)S(1)}, f32[384,128]{1,0:T(8,128)S(1)}, u32[]{:S(2)}, u32[]{:S(2)}) collective-permute-start(f32[384,128]{1,0:T(8,128)S(1)} %get-tuple-element.47.thin), channel_id=1, source_target_pairs={{4,2},{12,10},{20,18},{28,26},{36,34},{44,42},{52,50},{60,58},{68,... | collective-permute-start | bytes 589832 | tf_op jit(solution)/shard_map/ppermute | solution.py:399
  22.1 0.0 collective-permute-done.5.full
  22.1 1.3 %collective-permute-start.7 = (f32[256,384]{1,0:T(8,128)S(1)}, f32[256,384]{1,0:T(8,128)S(1)}, u32[]{:S(2)}, u32[]{:S(2)}) collective-permute-start(f32[256,384]{1,0:T(8,128)S(1)} %get-tuple-element.52), channel_id=1, source_target_pairs={{10,7},{11,6},{18,15},{19,14},{26,23},{27,22},{34,31},{35,30},{42,... | collective-permute-start | bytes 1179656 | tf_op jit(solution)/shard_map/ppermute | solution.py:454
  23.4 0.0 collective-permute-done.6.thin_in
  23.4 1.3 %collective-permute-start.8 = (f32[384,128]{1,0:T(8,128)S(1)}, f32[384,128]{1,0:T(8,128)S(1)}, u32[]{:S(2)}, u32[]{:S(2)}) collective-permute-start(f32[384,128]{1,0:T(8,128)S(1)} %get-tuple-element.55), channel_id=1, source_target_pairs={{10,6},{18,14},{26,22},{34,30},{42,38},{50,46},{58,54},{66,62},{74... | collective-permute-start | bytes 589832 | tf_op jit(solution)/shard_map/ppermute | solution.py:399
  24.7 11.3 %collective-permute-done.2.u_left = f32[384,384]{1,0:T(8,128)S(1)} collective-permute-done((f32[384,384]{1,0:T(8,128)S(1)}, f32[384,384]{1,0:T(8,128)S(1)}, u32[]{:S(2)}, u32[]{:S(2)}) %collective-permute-start.2) | collective-permute-done | bytes 589856 | tf_op jit(solution)/shard_map/ppermute | solution.py:399
  36.0 0.0 collective-permute-done.1.full
  36.0 4.0 %shard_map.53 = (f32[384,896]{1,0:T(8,128)S(1)}, f32[384,384]{1,0:T(8,128)S(1)}, f32[384,128]{1,0:T(8,128)S(1)}) custom-call(f32[384,896]{1,0:T(8,128)S(1)} %collective-permute-done.1.full, f32[384,384]{1,0:T(8,128)S(1)} %collective-permute-done.2.u_left, f32[384,896]{1,0:T(8,128)S(1)} %get-tuple-element.30.pay, f32[384,896]{1,0:T(8,128)S(1)} %collective-permute-done.recv, ...), custom_call_target="tpu_custom_call" | custom-call | flops 2378170368 | bytes 4194304 | tf_op jit(solution)/shard_map/pallas_call | solution.py:465
  40.0 2.3 %collective-permute-done.3.packed_in = f32[384,384]{1,0:T(8,128)S(1)} collective-permute-done((f32[384,384]{1,0:T(8,128)S(1)}, f32[384,384]{1,0:T(8,128)S(1)}, u32[]{:S(2)}, u32[]{:S(2)}) %collective-permute-start.3) | collective-permute-done | bytes 589856 | tf_op jit(solution)/shard_map/ppermute | solution.py:399
  42.3 4.6 %shard_map.56 = (f32[384,384]{1,0:T(8,128)S(1)}, f32[384,128]{1,0:T(8,128)S(1)}, bf16[384,1536]{1,0:T(8,128)(2,1)S(1)}, f32[2,384,384]{2,1,0:T(8,128)}, f32[2,384,128]{2,1,0:T(8,128)}) custom-call(f32[384,384]{1,0:T(8,128)S(1)} %get-tuple-element.39.whole, f32[384,128]{1,0:T(8,128)S(1)} %get-tuple-element.40.thin, ...), custom_call_target="tpu_custom_call", output_to_operand_aliasing={{3}: (7, {}), {4}: (8, {})} | custom-call | flops 2150545408 | bytes 4194304 | tf_op jit(solution)/shard_map/pallas_call | solution.py:473
  46.9 4.0 %shard_map.57.x_in = f32[384,384]{1,0:T(8,128)S(1)} custom-call(f32[384,384]{1,0:T(8,128)S(1)} %get-tuple-element.51.whole, f32[256,384]{1,0:T(8,128)S(1)} %collective-permute-done.7.packed_in, bf16[384,1536]{1,0:T(8,128)(2,1)S(1)} %get-tuple-element.53.u_both), custom_call_target="tpu_custom_call" | custom-call | flops 2038431744 | bytes 4194304 | tf_op jit(solution)/shard_map/pallas_call | solution.py:482
  50.9 0.0 collective-permute-done.8.thin_in
  51.0 1.2 %shard_map.58 = (f32[2,384,384]{2,1,0:T(8,128)}, f32[2,384,128]{2,1,0:T(8,128)}) custom-call(f32[384,384]{1,0:T(8,128)S(1)} %shard_map.57.x_in, f32[384,128]{1,0:T(8,128)S(1)} %get-tuple-element.54.thin, f32[384,128]{1,0:T(8,128)S(1)} %collective-permute-done.8.thin_in, ...), custom_call_target="tpu_custom_call", output_to_operand_aliasing={{0}: (4, {}), {1}: (5, {})} | custom-call | flops 112113744 | bytes 4194304 | tf_op jit(solution)/shard_map/pallas_call | solution.py:490
  (3 shorter events, 0.0 us)
Async XLA Ops:
  6.5 5.4 %collective-permute-start = (f32[384,896]{1,0:T(8,128)S(1)}, f32[384,896]{1,0:T(8,128)S(1)}, u32[]{:S(2)}, u32[]{:S(2)}) collective-permute-start(f32[384,896]{1,0:T(8,128)S(1)} %get-tuple-element.30.pay), channel_id=1, source_target_pairs={{0,2},{2,0},{4,6},{6,4},{8,10},{10,8},{12,14},{14,12},{16,18},{18,... | collective-permute-start | bytes 4128776 | tf_op jit(solution)/shard_map/ppermute | solution.py:399
  16.0 6.0 %collective-permute-start.5 = (f32[384,896]{1,0:T(8,128)S(1)}, f32[384,896]{1,0:T(8,128)S(1)}, u32[]{:S(2)}, u32[]{:S(2)}) collective-permute-start(f32[384,896]{1,0:T(8,128)S(1)} %get-tuple-element.37), channel_id=1, source_target_pairs={{0,2},{8,10},{16,18},{24,26},{32,34},{40,42},{48,50},{56,58},{64,6... | collective-permute-start | bytes 4128776 | tf_op jit(solution)/shard_map/ppermute | solution.py:399
  16.8 19.2 %collective-permute-start.1 = (f32[384,896]{1,0:T(8,128)S(1)}, f32[384,896]{1,0:T(8,128)S(1)}, u32[]{:S(2)}, u32[]{:S(2)}) collective-permute-start(f32[384,896]{1,0:T(8,128)S(1)} %get-tuple-element.37), channel_id=1, source_target_pairs={{4,6},{12,14},{20,22},{28,30},{36,38},{44,46},{52,54},{60,62},{68,... | collective-permute-start | bytes 4128776 | tf_op jit(solution)/shard_map/ppermute | solution.py:399
  18.1 3.3 %collective-permute-start.4 = (f32[256,384]{1,0:T(8,128)S(1)}, f32[256,384]{1,0:T(8,128)S(1)}, u32[]{:S(2)}, u32[]{:S(2)}) collective-permute-start(f32[256,384]{1,0:T(8,128)S(1)} %get-tuple-element.44), channel_id=1, source_target_pairs={{4,2},{12,10},{20,18},{28,26},{36,34},{44,42},{52,50},{60,58},{68,... | collective-permute-start | bytes 1179656 | tf_op jit(solution)/shard_map/ppermute | solution.py:399
  18.8 17.2 %collective-permute-start.2 = (f32[384,384]{1,0:T(8,128)S(1)}, f32[384,384]{1,0:T(8,128)S(1)}, u32[]{:S(2)}, u32[]{:S(2)}) collective-permute-start(f32[384,384]{1,0:T(8,128)S(1)} %get-tuple-element.38.u_high), channel_id=1, source_target_pairs={{2,6},{10,14},{18,22},{26,30},{34,38},{42,46},{50,54},{58,62},{66,... | collective-permute-start | bytes 1769480 | tf_op jit(solution)/shard_map/ppermute | solution.py:399
  20.1 22.3 %collective-permute-start.3 = (f32[384,384]{1,0:T(8,128)S(1)}, f32[384,384]{1,0:T(8,128)S(1)}, u32[]{:S(2)}, u32[]{:S(2)}) collective-permute-start(f32[384,384]{1,0:T(8,128)S(1)} %get-tuple-element.41), channel_id=1, source_target_pairs={{2,6},{10,14},{18,22},{26,30},{34,38},{42,46},{50,54},{58,62},{66,... | collective-permute-start | bytes 1769480 | tf_op jit(solution)/shard_map/ppermute | solution.py:399
  21.4 2.0 %collective-permute-start.6 = (f32[384,128]{1,0:T(8,128)S(1)}, f32[384,128]{1,0:T(8,128)S(1)}, u32[]{:S(2)}, u32[]{:S(2)}) collective-permute-start(f32[384,128]{1,0:T(8,128)S(1)} %get-tuple-element.47.thin), channel_id=1, source_target_pairs={{4,2},{12,10},{20,18},{28,26},{36,34},{44,42},{52,50},{60,58},{68,... | collective-permute-start | bytes 589832 | tf_op jit(solution)/shard_map/ppermute | solution.py:399
  22.1 24.8 %collective-permute-start.7 = (f32[256,384]{1,0:T(8,128)S(1)}, f32[256,384]{1,0:T(8,128)S(1)}, u32[]{:S(2)}, u32[]{:S(2)}) collective-permute-start(f32[256,384]{1,0:T(8,128)S(1)} %get-tuple-element.52), channel_id=1, source_target_pairs={{10,7},{11,6},{18,15},{19,14},{26,23},{27,22},{34,31},{35,30},{42,... | collective-permute-start | bytes 1179656 | tf_op jit(solution)/shard_map/ppermute | solution.py:454
  23.4 27.5 %collective-permute-start.8 = (f32[384,128]{1,0:T(8,128)S(1)}, f32[384,128]{1,0:T(8,128)S(1)}, u32[]{:S(2)}, u32[]{:S(2)}) collective-permute-start(f32[384,128]{1,0:T(8,128)S(1)} %get-tuple-element.55), channel_id=1, source_target_pairs={{10,6},{18,14},{26,22},{34,30},{42,38},{50,46},{58,54},{66,62},{74... | collective-permute-start | bytes 589832 | tf_op jit(solution)/shard_map/ppermute | solution.py:399
